TPU v7x, 32 devices: a whole 2x2x4 slice. The times are simulated.
32 devices in a mesh: rep: 2 (over y), seq: 4 (over z), head: 2 (over x), sub: 2 (over core).
Axes of the slice: x: 2, y: 2, z: 4, core: 2. Of those that a mesh axis runs over, the one named last changes fastest.
Arguments:
- key_cache: float32 [8, 32768, 128], P('head', ('rep', 'seq')), parts along dimension 1, may hold values from -40 to 40
- value_cache: bfloat16 [8, 32768, 128], P('head', ('rep', 'seq')), parts along dimension 1, may hold values from -6 to 6
- centroids: float32 [8, 1024, 128], P('head', ('rep', 'sub')), parts along dimension 1, may hold values from -8 to 8
- inv_temp: float32 [8], P('head'), may hold values from 0.015625 to 0.078125
- page_owner: int32 [8, 256, 1], P('head', ('rep', 'seq')), parts along dimension 1, may hold values from 0 to 3; in each aligned block of 32 rows (0 to 31, 32 to 63, ..., all dimensions but the last counted through in order) at most 12 rows name the same one
Outputs:
- clusters: float32 [8, 1024, 128], P('head', ('rep', 'sub')), parts along dimension 1
- moved_keys: bfloat16 [8, 384, 128, 128], P('head', ('rep', 'seq')), parts along dimension 1
- moved_values: bfloat16 [8, 384, 128, 128], P('head', ('rep', 'seq')), parts along dimension 1
- page_ids: int32 [8, 384], P('head', ('rep', 'seq')), parts along dimension 1
There are 2 independent parts, one for each index of `rep`. A program takes and returns all parts, laid end to end along the dimension named above; an argument that names none is the same for every part. Nothing has to cross between parts.
Inputs may be any that keep to these rules, and one draw needn't show every extreme that they name: `page_owner`: among the 32 pages of one head on one index of seq (an aligned block), no owner is named by more than 12 pages, a bound that some block reaches.
All inputs are finite; a program needn't handle non-finite values.
Results may differ from a plain program's by a relative error of at most 0.0075.
Values may be sent and summed in bfloat16 or wider, within the bound.
No kernel may reach another device: no remote copies, remote signals or barrier semaphores. Data moves between devices by JAX's collectives and lax.ppermute only.
A program may use at most 128 MiB of HBM per device.

v0:
```python
import functools

import jax
import jax.numpy as jnp
from jax import lax
from jax.experimental import pallas as pl
from jax.experimental.pallas import tpu as pltpu
from jax.sharding import PartitionSpec as P


ITERS = 3
PAGE = 128
PRIOR = 8.0
TAIL = 16
LOG2E = 1.4426950408889634


def chunk_plan(ranks, heads, capacity):
    plan = []
    for head in range(heads):
        for shift in range(1, ranks):
            crossing = min(shift, ranks - shift)
            pieces = crossing if capacity % crossing == 0 else 1
            for piece in range(pieces):
                plan.append((shift, head, piece * (capacity // pieces), capacity // pieces))
    return plan


def fill_table(owner_ref, table_ref, count_ref, head, ranks, capacity, pages):
    def clear(slot, carry):
        table_ref[slot] = pages
        return carry

    lax.fori_loop(0, ranks * capacity, clear, 0)
    for rank in range(ranks):
        count_ref[rank] = 0

    def put(page, carry):
        owner = owner_ref[head, page]
        place = count_ref[owner]
        table_ref[owner * capacity + place] = page
        count_ref[owner] = place + 1
        return carry

    lax.fori_loop(0, pages, put, 0)


def scatter_kernel(plan, ranks, capacity, pages, with_cast, owner_ref, cache_ref, *refs):
    chunk_refs, refs = refs[: len(plan)], refs[len(plan) :]
    if with_cast:
        low_ref, local_ref, wide_ref, page_ref, table_ref, count_ref, in_sem, chunk_sem, local_sem, low_sem = refs
    else:
        local_ref, page_ref, table_ref, count_ref, in_sem, chunk_sem, local_sem = refs
    heads = cache_ref.shape[0]
    me = lax.axis_index("seq")
    core = lax.axis_index("sub")
    share = heads // lax.axis_size("sub")
    order = [(core * share + i) for i in range(share)]
    order += [lax.rem(core * share + i, heads) for i in range(share, heads)]
    into = wide_ref if with_cast else page_ref
    loads = []
    for i, head in enumerate(order):
        target = into.at[i] if with_cast else into.at[i, pl.ds(0, pages)]
        load = pltpu.make_async_copy(cache_ref.at[head], target, in_sem.at[i])
        load.start()
        loads.append(load)
    for i in range(heads):
        page_ref[i, pages] = jnp.zeros(page_ref.shape[2:], page_ref.dtype)
    for i, head in enumerate(order):
        fill_table(owner_ref, table_ref, count_ref, head, ranks, capacity, pages)
        loads[i].wait()
        if with_cast:

            def cast(page, carry, i=i):
                page_ref[i, page] = wide_ref[i, page].astype(page_ref.dtype)
                return carry

            lax.fori_loop(0, pages, cast, 0, unroll=2)
            if i < share:
                pltpu.make_async_copy(page_ref.at[i, pl.ds(0, pages)], low_ref.at[i], low_sem.at[i]).start()
        for j, (shift, chunk_head, first, size) in enumerate(plan):
            if chunk_head != i:
                continue
            base = lax.rem(me + shift, ranks) * capacity + first

            def send(slot, carry, i=i, j=j, base=base):
                page = table_ref[base + slot]
                pltpu.make_async_copy(page_ref.at[i, page], chunk_refs[j].at[slot], chunk_sem.at[j]).start()
                return carry

            lax.fori_loop(0, size, send, 0)

        def keep(slot, carry, i=i, head=head):
            place = me * capacity + slot
            page = table_ref[place]
            pltpu.make_async_copy(page_ref.at[i, page], local_ref.at[head, place], local_sem).start()
            return carry

        lax.fori_loop(0, capacity, keep, 0)
    for j in range(len(plan)):
        pltpu.make_async_copy(chunk_refs[j], chunk_refs[j], chunk_sem.at[j]).wait()
    if with_cast:
        for i in range(share):
            pltpu.make_async_copy(low_ref.at[i], low_ref.at[i], low_sem.at[i]).wait()
    kept = local_ref.at[:, pl.ds(0, capacity)]
    pltpu.make_async_copy(kept, kept, local_sem).wait()


def scatter_pages(owner, cache, plan, ranks, capacity, with_cast):
    heads, tokens, width = cache.shape
    pages = tokens // PAGE
    share = heads // lax.axis_size("sub")
    page_shape = (PAGE, width)
    low = jnp.bfloat16
    anywhere = pl.BlockSpec(memory_space=pl.ANY)
    out_shape = [jax.ShapeDtypeStruct((size,) + page_shape, low) for _, _, _, size in plan]
    if with_cast:
        out_shape.append(jax.ShapeDtypeStruct((share, pages) + page_shape, low))
    out_shape.append(jax.ShapeDtypeStruct((heads, ranks * capacity) + page_shape, low))
    scratch = []
    if with_cast:
        scratch.append(pltpu.VMEM((heads, pages) + page_shape, cache.dtype))
    scratch += [
        pltpu.VMEM((heads, pages + 1) + page_shape, low),
        pltpu.SMEM((ranks * capacity,), jnp.int32),
        pltpu.SMEM((ranks,), jnp.int32),
        pltpu.SemaphoreType.DMA((heads,)),
        pltpu.SemaphoreType.DMA((len(plan),)),
        pltpu.SemaphoreType.DMA,
    ]
    if with_cast:
        scratch.append(pltpu.SemaphoreType.DMA((share,)))
    return pl.pallas_call(
        functools.partial(scatter_kernel, plan, ranks, capacity, pages, with_cast),
        out_shape=out_shape,
        in_specs=[pl.BlockSpec(memory_space=pltpu.SMEM), anywhere],
        out_specs=[anywhere] * len(out_shape),
        scratch_shapes=scratch,
        name="scatter_keys" if with_cast else "scatter_values",
        cost_estimate=pl.CostEstimate(flops=0, bytes_accessed=16 << 20, transcendentals=0),
    )(owner, cache.reshape((heads, pages) + page_shape))


def tail_rows(first, second, dtype):
    rows = lax.broadcasted_iota(jnp.int32, (TAIL, PAGE), 0)
    return jnp.where(rows == 0, first, jnp.where(rows == 1, second, 0.0)).astype(dtype)


def split_mass(mass):
    high = mass.astype(jnp.bfloat16).astype(jnp.float32)
    rows = lax.broadcasted_iota(jnp.int32, mass.shape, 0)
    blocks = mass.shape[0] // 2
    held = jnp.where(rows < blocks // 4, high, 0.0)
    rest = jnp.where(rows < blocks // 4, mass - high, 0.0)
    return (held + pltpu.roll(rest, blocks // 4, 0)).astype(jnp.bfloat16)


def join_mass(tail):
    wide = tail.astype(jnp.float32)
    return wide + pltpu.roll(wide, TAIL - TAIL // 8, 0)


def sweep_kernel(tile, temp_ref, keys_ref, own_ref, other_ref, keep_ref, send_ref, sums_ref, table_ref):
    half, width = own_ref.shape[1:]
    core = lax.axis_index("sub")
    rate = temp_ref[core * pl.num_programs(0) + pl.program_id(0)] * LOG2E
    lane = lax.broadcasted_iota(jnp.int32, (half, width), 1)
    for part, ref in ((0, own_ref), (1, other_ref)):
        table = ref[0]
        norm = -0.5 * jnp.sum(table * table, axis=1, keepdims=True)
        high = norm.astype(jnp.bfloat16).astype(jnp.float32)
        mid = (norm - high).astype(jnp.bfloat16).astype(jnp.float32)
        low = norm - high - mid
        extra = jnp.where(lane == 0, high, jnp.where(lane == 1, mid, jnp.where(lane == 2, low, 0.0)))
        rows = pl.ds(part * half, half)
        table_ref[rows, 0:width] = table.astype(jnp.bfloat16)
        table_ref[rows, width : 2 * width] = extra.astype(jnp.bfloat16)
    sums_ref[...] = jnp.zeros_like(sums_ref)

    def step(at, carry):
        keys = keys_ref[0, pl.ds(pl.multiple_of(at * tile, tile), tile), :]
        wide = jnp.concatenate([keys, jnp.ones_like(keys)], axis=1)
        scores = lax.dot_general(
            table_ref[...], wide, (((1,), (1,)), ((), ())), preferred_element_type=jnp.float32
        )
        highest = jnp.max(scores, axis=0, keepdims=True)
        spread = jnp.exp2((scores - highest) * rate)
        total = jnp.sum(spread, axis=0, keepdims=True)
        weights = (spread * (1.0 / total)).astype(jnp.bfloat16)
        sums_ref[...] += jnp.dot(weights, wide, preferred_element_type=jnp.float32)
        return carry

    lax.fori_loop(0, keys_ref.shape[1] // tile, step, 0, unroll=2)
    masses = []
    for block in range(2 * half // width):
        masses.append(jnp.transpose(sums_ref[pl.ds(block * width, width), width : 2 * width])[0:TAIL])
    keep_ref[0, 0:half] = sums_ref[0:half, 0:width]
    keep_ref[0, half : half + TAIL] = tail_rows(masses[0], masses[1], jnp.float32)
    send_ref[0, 0:half] = sums_ref[half : 2 * half, 0:width].astype(jnp.bfloat16)
    send_ref[0, half : half + TAIL] = split_mass(tail_rows(masses[2], masses[3], jnp.float32))


def sweep(temp, keys, own, other, tile):
    heads, tokens, width = keys.shape
    half = own.shape[1]
    table_spec = pl.BlockSpec((1, half, width), lambda h: (h, 0, 0))
    load_spec = pl.BlockSpec((1, half + TAIL, width), lambda h: (h, 0, 0))
    return pl.pallas_call(
        functools.partial(sweep_kernel, tile),
        grid=(heads,),
        in_specs=[
            pl.BlockSpec(memory_space=pltpu.SMEM),
            pl.BlockSpec((1, tokens, width), lambda h: (h, 0, 0)),
            table_spec,
            table_spec,
        ],
        out_specs=[load_spec, load_spec],
        out_shape=[
            jax.ShapeDtypeStruct((heads, half + TAIL, width), jnp.float32),
            jax.ShapeDtypeStruct((heads, half + TAIL, width), jnp.bfloat16),
        ],
        scratch_shapes=[
            pltpu.VMEM((2 * half, 2 * width), jnp.float32),
            pltpu.VMEM((2 * half, 2 * width), jnp.bfloat16),
        ],
        name="sweep",
        cost_estimate=pl.CostEstimate(
            flops=8 * heads * tokens * half * width, bytes_accessed=2 * heads * tokens * width, transcendentals=2 * heads * tokens * half
        ),
    )(temp, keys, own, other)


def join_kernel(left_ref, right_ref, out_ref):
    half = left_ref.shape[1] - TAIL
    for head in range(left_ref.shape[0]):
        body = left_ref[head, 0:half].astype(jnp.float32) + right_ref[head, 0:half].astype(jnp.float32)
        out_ref[head, 0:half] = body.astype(jnp.bfloat16)
        if left_ref.dtype == jnp.float32:
            mass = left_ref[head, half : half + TAIL]
        else:
            mass = join_mass(left_ref[head, half : half + TAIL])
        mass = mass + join_mass(right_ref[head, half : half + TAIL])
        out_ref[head, half : half + TAIL] = split_mass(mass)


def join(left, right):
    return pl.pallas_call(
        join_kernel,
        out_shape=jax.ShapeDtypeStruct(left.shape, jnp.bfloat16),
        name="join",
    )(left, right)


def renew_kernel(left_ref, right_ref, table_ref, out_ref):
    half, width = table_ref.shape[1:]
    for head in range(left_ref.shape[0]):
        mass = join_mass(left_ref[head, half : half + TAIL]) + join_mass(right_ref[head, half : half + TAIL])
        for block in range(half // width):
            rows = slice(block * width, (block + 1) * width)
            spread = jnp.transpose(jnp.broadcast_to(mass[block : block + 1], (width, width)))
            body = left_ref[head, rows].astype(jnp.float32) + right_ref[head, rows].astype(jnp.float32)
            out_ref[head, rows] = (body + PRIOR * table_ref[head, rows]) / (spread + PRIOR)


def renew(left, right, table):
    return pl.pallas_call(
        renew_kernel,
        out_shape=jax.ShapeDtypeStruct(table.shape, table.dtype),
        name="renew",
    )(left, right, table)


def tied(value, *others):
    return lax.optimization_barrier((value,) + others)


def lower_kernel(cores, cache_ref, *refs):
    ranks = cache_ref.shape[0]
    out_refs, (wide_ref, low_ref, in_sem, out_sem) = refs[:ranks], refs[ranks:]
    part = cache_ref.shape[1] // cores
    first = lax.axis_index("sub") * part
    me = lax.axis_index("seq")
    order = list(range(1, ranks)) + [0]
    for bit in order:
        pltpu.make_async_copy(
            cache_ref.at[me ^ bit, pl.ds(first, part)], wide_ref.at[bit], in_sem.at[bit]
        ).start()
    for bit in order:
        pltpu.make_async_copy(wide_ref.at[bit], wide_ref.at[bit], in_sem.at[bit]).wait()

        def cast(page, carry, bit=bit):
            low_ref[bit, page] = wide_ref[bit, page].astype(low_ref.dtype)
            return carry

        lax.fori_loop(0, part, cast, 0, unroll=2)
        pltpu.make_async_copy(low_ref.at[bit], out_refs[bit], out_sem.at[bit]).start()
    for bit in order:
        pltpu.make_async_copy(low_ref.at[bit], out_refs[bit], out_sem.at[bit]).wait()


def lower_keys(cache, cores):
    ranks, pages = cache.shape[:2]
    part = (pages // cores,) + cache.shape[2:]
    anywhere = pl.BlockSpec(memory_space=pl.ANY)
    return pl.pallas_call(
        functools.partial(lower_kernel, cores),
        out_shape=[jax.ShapeDtypeStruct(part, jnp.bfloat16)] * ranks,
        in_specs=[anywhere],
        out_specs=[anywhere] * ranks,
        scratch_shapes=[
            pltpu.VMEM((ranks,) + part, cache.dtype),
            pltpu.VMEM((ranks,) + part, jnp.bfloat16),
            pltpu.SemaphoreType.DMA((ranks,)),
            pltpu.SemaphoreType.DMA((ranks,)),
        ],
        name="lower_keys",
    )(cache)


def value_heads(me, bit):
    return [0, 1, 2, 3]


def near_pair(me, bit):
    base = ((me ^ 3) >> 1) << 1
    return [base, base + 1]


def near_one(me, bit):
    return [me]


def far_pair(me, bit):
    base = (me >> 1) << 1
    return [base, base + 1]


VALUE_PLAN = ((1, value_heads, 4), (2, value_heads, 4), (3, value_heads, 4))
KEY_PLAN = ((1, near_pair, 2), (1, near_one, 1), (2, far_pair, 2), (3, far_pair, 2))


def pack_kernel(plan, capacity, with_cast, owner_ref, cache_ref, *refs):
    chunk_refs, refs = refs[: len(plan)], refs[len(plan) :]
    if with_cast:
        local_ref, wide_ref, page_ref, table_ref, count_ref, in_sem, chunk_sem, local_sem = refs
    else:
        local_ref, page_ref, table_ref, count_ref, in_sem, chunk_sem, local_sem = refs
    ranks, pages = cache_ref.shape[:2]
    me = lax.axis_index("seq")
    core = lax.axis_index("sub")
    half = capacity // lax.axis_size("sub")
    loads = []
    for head in range(ranks):
        target = wide_ref.at[head] if with_cast else page_ref.at[head, pl.ds(0, pages)]
        load = pltpu.make_async_copy(cache_ref.at[head], target, in_sem.at[head])
        load.start()
        loads.append(load)
    for head in range(ranks):
        page_ref[head, pages] = jnp.zeros(page_ref.shape[2:], page_ref.dtype)
        fill_table(owner_ref, table_ref.at[head], count_ref, head, ranks, capacity, pages)
    for head in range(ranks):
        loads[head].wait()
        if with_cast:

            def cast(page, carry, head=head):
                page_ref[head, page] = wide_ref[head, page].astype(page_ref.dtype)
                return carry

            lax.fori_loop(0, pages, cast, 0, unroll=2)
    for at, (bit, heads_of, _) in enumerate(plan):
        for i, head in enumerate(heads_of(me, bit)):

            def send(slot, carry, at=at, i=i, head=head, bit=bit):
                page = table_ref[head, (me ^ bit) * capacity + core * half + slot]
                pltpu.make_async_copy(page_ref.at[head, page], chunk_refs[at].at[i, slot], chunk_sem.at[at]).start()
                return carry

            lax.fori_loop(0, half, send, 0)
    for head in range(ranks):

        def keep(slot, carry, head=head):
            place = me * capacity + slot
            page = table_ref[head, place]
            pltpu.make_async_copy(page_ref.at[head, page], local_ref.at[head, place], local_sem).start()
            return carry

        lax.fori_loop(0, capacity, keep, 0)
    for at in range(len(plan)):
        pltpu.make_async_copy(chunk_refs[at], chunk_refs[at], chunk_sem.at[at]).wait()
    kept = local_ref.at[:, pl.ds(0, capacity)]
    pltpu.make_async_copy(kept, kept, local_sem).wait()


def pack_pages(owner, cache, plan, capacity, with_cast):
    ranks, pages = cache.shape[:2]
    page_shape = cache.shape[2:]
    half = capacity // lax.axis_size("sub")
    low = jnp.bfloat16
    anywhere = pl.BlockSpec(memory_space=pl.ANY)
    out_shape = [jax.ShapeDtypeStruct((count, half) + page_shape, low) for _, _, count in plan]
    out_shape.append(jax.ShapeDtypeStruct((ranks, ranks * capacity) + page_shape, low))
    scratch = [pltpu.VMEM((ranks, pages) + page_shape, cache.dtype)] if with_cast else []
    scratch += [
        pltpu.VMEM((ranks, pages + 1) + page_shape, low),
        pltpu.SMEM((ranks, ranks * capacity), jnp.int32),
        pltpu.SMEM((ranks,), jnp.int32),
        pltpu.SemaphoreType.DMA((ranks,)),
        pltpu.SemaphoreType.DMA((len(plan),)),
        pltpu.SemaphoreType.DMA,
    ]
    return pl.pallas_call(
        functools.partial(pack_kernel, plan, capacity, with_cast),
        out_shape=out_shape,
        in_specs=[pl.BlockSpec(memory_space=pltpu.SMEM), anywhere],
        out_specs=[anywhere] * len(out_shape),
        scratch_shapes=scratch,
        name="pack_keys" if with_cast else "pack_values",
    )(owner, cache)


def home_kernel(capacity, *refs):
    owner_refs, own_refs, got_refs = refs[0:3], refs[3:6], refs[6:9]
    _, local_ref, next_ref, page_ref, table_ref, in_sem, local_sem, next_sem = refs[9:]
    part = own_refs[0].shape[0]
    pages = part * lax.axis_size("sub")
    me = lax.axis_index("seq")
    core = lax.axis_index("sub")
    for i in range(3):
        pltpu.make_async_copy(own_refs[i], page_ref.at[i, pl.ds(core * part, part)], in_sem.at[i]).start()
        pltpu.make_async_copy(got_refs[i], page_ref.at[i, pl.ds((1 - core) * part, part)], in_sem.at[3 + i]).start()
        page_ref[i, pages] = jnp.zeros(page_ref.shape[2:], page_ref.dtype)

    def clear(slot, carry):
        for row in range(6):
            table_ref[row, slot] = pages
        return carry

    lax.fori_loop(0, capacity, clear, 0)
    for i in range(3):

        def put(page, counts, i=i):
            mine, near = counts
            owner = owner_refs[i][me, page]
            for row, count, wanted in ((i, mine, me), (3 + i, near, me ^ 1)):

                @pl.when(owner == wanted)
                def _(row=row, count=count):
                    table_ref[row, count] = page

            return mine + jnp.where(owner == me, 1, 0), near + jnp.where(owner == (me ^ 1), 1, 0)

        lax.fori_loop(0, pages, put, (jnp.int32(0), jnp.int32(0)))
    for i in range(3):
        whole = page_ref.at[i, pl.ds(0, part)]
        pltpu.make_async_copy(whole, whole, in_sem.at[i]).wait()
        pltpu.make_async_copy(whole, whole, in_sem.at[3 + i]).wait()

    def relay(slot, carry):
        page = table_ref[4 + core, slot]
        pltpu.make_async_copy(page_ref.at[1 + core, page], next_ref.at[slot], next_sem).start()
        return carry

    lax.fori_loop(0, capacity, relay, 0)
    for i in range(3):

        def keep(slot, carry, i=i):
            page = table_ref[i, slot]
            place = (me ^ (i + 1)) * capacity + slot
            pltpu.make_async_copy(page_ref.at[i, page], local_ref.at[me, place], local_sem).start()
            return carry

        lax.fori_loop(0, capacity, keep, 0)
    pltpu.make_async_copy(next_ref, next_ref, next_sem).wait()
    kept = local_ref.at[0, pl.ds(0, 3 * capacity)]
    pltpu.make_async_copy(kept, kept, local_sem).wait()


def home_pages(owners, own, got, local, capacity):
    page_shape = local.shape[2:]
    pages = own[0].shape[0] * lax.axis_size("sub")
    anywhere = pl.BlockSpec(memory_space=pl.ANY)
    return pl.pallas_call(
        functools.partial(home_kernel, capacity),
        out_shape=[
            jax.ShapeDtypeStruct(local.shape, local.dtype),
            jax.ShapeDtypeStruct((capacity,) + page_shape, local.dtype),
        ],
        in_specs=[pl.BlockSpec(memory_space=pltpu.SMEM)] * 3 + [anywhere] * 7,
        out_specs=[anywhere] * 2,
        scratch_shapes=[
            pltpu.VMEM((3, pages + 1) + page_shape, local.dtype),
            pltpu.SMEM((6, capacity), jnp.int32),
            pltpu.SemaphoreType.DMA((6,)),
            pltpu.SemaphoreType.DMA,
            pltpu.SemaphoreType.DMA,
        ],
        input_output_aliases={9: 0},
        name="home_pages",
    )(*owners, *own, *got, local)


def home_sweep_kernel(tile, temp_ref, *refs):
    key_refs, (center_ref, out_ref, sums_ref, table_ref) = refs[:-4], refs[-4:]
    count, width = center_ref.shape
    rate = temp_ref[lax.axis_index("seq")] * LOG2E
    table = center_ref[...]
    lane = lax.broadcasted_iota(jnp.int32, table.shape, 1)
    norm = -0.5 * jnp.sum(table * table, axis=1, keepdims=True)
    high = norm.astype(jnp.bfloat16).astype(jnp.float32)
    mid = (norm - high).astype(jnp.bfloat16).astype(jnp.float32)
    low = norm - high - mid
    extra = jnp.where(lane == 0, high, jnp.where(lane == 1, mid, jnp.where(lane == 2, low, 0.0)))
    table_ref[:, 0:width] = table.astype(jnp.bfloat16)
    table_ref[:, width : 2 * width] = extra.astype(jnp.bfloat16)
    sums_ref[...] = jnp.zeros_like(sums_ref)
    for keys_ref in key_refs:

        def step(at, carry, keys_ref=keys_ref):
            keys = keys_ref[pl.ds(pl.multiple_of(at * tile, tile), tile), :]
            wide = jnp.concatenate([keys, jnp.ones_like(keys)], axis=1)
            scores = lax.dot_general(
                table_ref[...], wide, (((1,), (1,)), ((), ())), preferred_element_type=jnp.float32
            )
            highest = jnp.max(scores, axis=0, keepdims=True)
            spread = jnp.exp2((scores - highest) * rate)
            total = jnp.sum(spread, axis=0, keepdims=True)
            weights = (spread * (1.0 / total)).astype(jnp.bfloat16)
            sums_ref[...] += jnp.dot(weights, wide, preferred_element_type=jnp.float32)
            return carry

        lax.fori_loop(0, keys_ref.shape[0] // tile, step, 0, unroll=2)
    out_ref[0:count] = sums_ref[:, 0:width]
    rows = lax.broadcasted_iota(jnp.int32, (TAIL, width), 0)
    tail = jnp.zeros((TAIL, width), jnp.float32)
    for block in range(count // width):
        mass = jnp.transpose(sums_ref[pl.ds(block * width, width), width : 2 * width])[0:TAIL]
        tail = jnp.where(rows == block, mass, tail)
    out_ref[count : count + TAIL] = tail


def home_sweep(temp, keys, table, tile):
    count, width = table.shape
    vmem = pl.BlockSpec(memory_space=pltpu.VMEM)
    return pl.pallas_call(
        functools.partial(home_sweep_kernel, tile),
        out_shape=jax.ShapeDtypeStruct((count + TAIL, width), jnp.float32),
        in_specs=[pl.BlockSpec(memory_space=pltpu.SMEM)] + [vmem] * (len(keys) + 1),
        out_specs=vmem,
        scratch_shapes=[
            pltpu.VMEM((count, 2 * width), jnp.float32),
            pltpu.VMEM((count, 2 * width), jnp.bfloat16),
        ],
        name="home_sweep",
    )(temp, *keys, table)


def home_renew_kernel(left_ref, right_ref, table_ref, out_ref):
    count, width = table_ref.shape
    mass = left_ref[count : count + TAIL] + right_ref[count : count + TAIL]
    for block in range(count // width):
        rows = slice(block * width, (block + 1) * width)
        spread = jnp.transpose(jnp.broadcast_to(mass[block : block + 1], (width, width)))
        body = left_ref[rows] + right_ref[rows]
        out_ref[rows] = (body + PRIOR * table_ref[rows]) / (spread + PRIOR)


def home_renew(left, right, table):
    return pl.pallas_call(
        home_renew_kernel, out_shape=jax.ShapeDtypeStruct(table.shape, table.dtype), name="home_renew"
    )(left, right, table)


def on_home_chips(key_cache, value_cache, centroids, inv_temp, page_owner):
    heads, tokens, width = key_cache.shape
    pages = tokens // PAGE
    ranks, cores = lax.axis_size("seq"), lax.axis_size("sub")
    me, core = lax.axis_index("seq"), lax.axis_index("sub")
    capacity = max(2, (3 * pages + 2 * ranks - 1) // (2 * ranks))
    half = capacity // cores
    owner = page_owner[:, :, 0]
    paged = (heads, pages, PAGE, width)

    def across(value):
        return lax.ppermute(value, "sub", [(0, 1), (1, 0)])

    def facing(value, bit):
        return lax.ppermute(value, "seq", [(i, i ^ bit) for i in range(ranks)])

    lowered = lower_keys(key_cache.reshape(paged), cores)
    homed = [lowered[0]] + [None] * 3
    for bit in range(1, ranks):
        homed[bit] = facing(lowered[bit], bit)

    owner_after, value_after = tied(owner, value_cache, lowered[1])[:2]
    *value_chunks, moved_values = pack_pages(owner_after, value_after.reshape(paged), VALUE_PLAN, capacity, False)
    values_in = [facing(value_chunks[i], VALUE_PLAN[i][0]) for i in range(len(VALUE_PLAN))]

    owner_after, key_after = tied(owner, key_cache, value_chunks[0])[:2]
    owners = [owner] + [facing(owner_after, bit) for bit in range(1, ranks)]
    *key_chunks, moved_keys = pack_pages(owner_after, key_after.reshape(paged), KEY_PLAN, capacity, True)
    keys_in = [facing(key_chunks[i], KEY_PLAN[i][0]) for i in range(len(KEY_PLAN) - 1)]

    seeds = lax.dynamic_index_in_dim(centroids, me, 0, keepdims=False)
    seeds_got = across(seeds)
    table = jnp.where(
        core == 0, jnp.concatenate([seeds, seeds_got], axis=0), jnp.concatenate([seeds_got, seeds], axis=0)
    )
    keys = [part.reshape(part.shape[0] * PAGE, width) for part in homed]
    for iteration in range(ITERS):
        sums = home_sweep(inv_temp, keys, table, 512)
        if iteration == 0:
            homed_got = [across(homed[bit]) for bit in (1, 2, 3)]
            moved_keys, relayed = home_pages(owners[1:], homed[1:], homed_got, moved_keys, capacity)
            relayed_in = facing(relayed, 1)
        table = home_renew(sums, across(sums), table)
        if iteration == 0:
            table, _ = tied(table, relayed)

    ours = lax.dynamic_slice_in_dim(table, core * (table.shape[0] // cores), table.shape[0] // cores, 0)
    opposite = facing(ours, 2)
    last, _ = tied(key_chunks[-1], table)
    keys_in.append(facing(last, KEY_PLAN[-1][0]))
    near = facing(jnp.stack([ours, opposite]), 1)

    def place(whole, part, head, slot):
        return lax.dynamic_update_slice(whole, part, (head, slot, 0, 0))

    def place_both(whole, part, bit, head):
        part, _ = tied(part, table)
        base = (me ^ bit) * capacity
        other = across(part)
        whole = place(whole, part, head, base + core * half)
        return place(whole, other, head, base + (1 - core) * half)

    for i, (bit, heads_of, _) in enumerate(VALUE_PLAN):
        moved_values = place_both(moved_values, values_in[i], bit, 0)
    for i, (bit, heads_of, _) in enumerate(KEY_PLAN):
        if i == len(KEY_PLAN) - 1:
            relayed_in, _ = tied(relayed_in, table)
            for part, side in ((relayed_in, core), (across(relayed_in), 1 - core)):
                moved_keys = place(moved_keys, part[None], me ^ 1, (me ^ 3 ^ side) * capacity)
        moved_keys = place_both(moved_keys, keys_in[i], bit, heads_of(me ^ bit, bit)[0])

    clusters = jnp.zeros(centroids.shape, centroids.dtype)
    for part, head in ((ours, me), (opposite, me ^ 2), (near[0], me ^ 1), (near[1], me ^ 3)):
        clusters = lax.dynamic_update_slice(clusters, part[None], (head, 0, 0))
    sources = [me ^ bit for bit in range(ranks)]
    return (clusters, moved_keys, moved_values, slot_pages(owners, sources, pages, capacity))


def slot_pages(owners, sources, pages, capacity):
    me = lax.axis_index("seq")
    slot_ids = jnp.arange(capacity, dtype=jnp.int32)
    heads = owners[0].shape[0]
    ids = jnp.full((heads, len(owners) * capacity), -1, jnp.int32)
    for owner, source in zip(owners, sources):
        hits = (owner == me).astype(jnp.int32)
        before = jnp.cumsum(hits, axis=1) - hits
        matched = (hits[:, None, :] == 1) & (before[:, None, :] == slot_ids[None, :, None])
        number = source * pages + jnp.arange(pages, dtype=jnp.int32)
        found = jnp.max(jnp.where(matched, number[None, None, :], -1), axis=2)
        ids = lax.dynamic_update_slice(ids, found, (0, source * capacity))
    return ids


def on_device(key_cache, value_cache, centroids, inv_temp, page_owner):
    heads, tokens, width = key_cache.shape
    pages = tokens // PAGE
    ranks = lax.axis_size("seq")
    cores = lax.axis_size("sub")
    me, core = lax.axis_index("seq"), lax.axis_index("sub")
    share = heads // cores
    capacity = max(2, (3 * pages + 2 * ranks - 1) // (2 * ranks))
    owner = page_owner[:, :, 0]
    swap = [(0, 1), (1, 0)]
    ring = lambda shift: [(i, (i + shift) % ranks) for i in range(ranks)]
    facing = lambda bit: [(i, i ^ bit) for i in range(ranks)]

    owners = [owner] + [lax.ppermute(owner, "seq", ring(shift)) for shift in range(1, ranks)]

    mine = lax.dynamic_slice_in_dim(centroids, core * share, share, 0)
    theirs = lax.dynamic_slice_in_dim(centroids, (1 - core) * share, share, 0)
    got = lax.ppermute(theirs, "sub", swap)
    straight = lax.rem(me, 2) == core
    own = jnp.where(straight, mine, got)
    other = jnp.where(straight, got, mine)

    plan = chunk_plan(ranks, share, capacity)
    *value_chunks, moved_values = scatter_pages(owner, value_cache, plan, ranks, capacity, False)
    *key_chunks, keys_low, moved_keys = scatter_pages(owner, key_cache, plan, ranks, capacity, True)
    keys_low = keys_low.reshape(share, tokens, width)

    waiting = [(0, spec, chunk) for spec, chunk in zip(plan, value_chunks)]
    waiting += [(1, spec, chunk) for spec, chunk in zip(plan, key_chunks)]
    moved = [moved_values, moved_keys]
    arrived = []

    def issue(count, after=None):
        for _ in range(count):
            if not waiting:
                return
            which, spec, chunk = waiting.pop(0)
            if after is not None:
                chunk, _ = tied(chunk, after)
            arrived.append((which, spec, lax.ppermute(chunk, "seq", ring(spec[0]))))

    stages = ITERS * (1 + ranks.bit_length())
    per_stage = -(-len(waiting) // (stages + 1))
    issue(2)
    for _ in range(ITERS):
        keep, send = sweep(inv_temp, keys_low, own, other, 512)
        got = lax.ppermute(send, "seq", facing(1))
        issue(per_stage, send)
        payload = join(keep, got)
        bit = 2
        while bit < ranks:
            got = lax.ppermute(payload, "seq", facing(bit))
            issue(per_stage, payload)
            bit *= 2
            if bit < ranks:
                payload = join(payload, got)
        own = renew(payload, got, own)
        other = lax.ppermute(own, "seq", facing(1))
        issue(per_stage, own)
    issue(len(waiting))

    for which, (shift, head, first, size), chunk in arrived:
        partner = lax.ppermute(chunk, "sub", swap)
        start = lax.rem(me - shift + ranks, ranks) * capacity + first
        place = lambda whole, part, at: lax.dynamic_update_slice(whole, part[None], (at, start, 0, 0))
        moved[which] = place(moved[which], chunk, core * share + head)
        moved[which] = place(moved[which], partner, (1 - core) * share + head)

    lower = jnp.where(lax.rem(me, 2) == 0, own, other)
    upper = jnp.where(lax.rem(me, 2) == 0, other, own)
    ours = jnp.where(core == 0, lower, upper)
    other_half = lax.ppermute(jnp.where(core == 0, upper, lower), "sub", swap)
    clusters = jnp.where(
        core == 0, jnp.concatenate([ours, other_half], axis=0), jnp.concatenate([other_half, ours], axis=0)
    )

    sources = [lax.rem(me - shift + ranks, ranks) for shift in range(ranks)]
    ids = slot_pages(owners, sources, pages, capacity)
    return (clusters, moved[1], moved[0], ids)


def choose(key_cache, value_cache, centroids, inv_temp, page_owner):
    ranks, cores = lax.axis_size("seq"), lax.axis_size("sub")
    homes = ranks == 4 and key_cache.shape[0] == ranks and cores == 2
    if not homes:
        return on_device(key_cache, value_cache, centroids, inv_temp, page_owner)
    return on_home_chips(key_cache, value_cache, centroids, inv_temp, page_owner)


def solution(mesh):
    return jax.shard_map(
        choose,
        mesh=mesh,
        in_specs=(
            P("head", ("rep", "seq"), None),
            P("head", ("rep", "seq"), None),
            P("head", ("rep", "sub"), None),
            P("head"),
            P("head", ("rep", "seq"), None),
        ),
        out_specs=(
            P("head", ("rep", "sub"), None),
            P("head", ("rep", "seq"), None, None),
            P("head", ("rep", "seq"), None, None),
            P("head", ("rep", "seq")),
        ),
        check_vma=False,
    )
```

profile of v0, /device:TPU:9, one launch (start us, length us, event | category | flops | bytes accessed | tf_op | source)
XLA Modules:
  0.0 218.2 jit_solution(703156512654777912)
XLA Ops:
  0.7 1.0 copy-done
  1.7 0.7 collective-permute-start.3
  2.4 3.1 %lower_keys.1 = (bf16[16,128,128]{2,1,0:T(8,128)(2,1)}, bf16[16,128,128]{2,1,0:T(8,128)(2,1)}, bf16[16,128,128]{2,1,0:T(8,128)(2,1)}, bf16[16,128,128]{2,1,0:T(8,128)(2,1)}) custom-call(f32[4,32,128,128]{3,2,1,0:T(8,128)} %bitcast.18), custom_call_target="tpu_custom_call" | custom-call | tf_op jit(solution)/shard_map/lower_keys/pallas_call | solution.py:305
  5.6 2.5 %collective-permute-start.1 = (bf16[16,128,128]{2,1,0:T(8,128)(2,1)}, bf16[16,128,128]{2,1,0:T(8,128)(2,1)S(1)}, u32[]{:S(2)}, u32[]{:S(2)}) collective-permute-start(bf16[16,128,128]{2,1,0:T(8,128)(2,1)} %get-tuple-element.35), channel_id=1, source_target_pairs={{0,8},{4,12},{8,0},{12,4},{1,9},{5,13},{9,1},{13,5},{2,10},{6,14},... | collective-permute-start | bytes 1572872 | tf_op jit(solution)/shard_map/ppermute | solution.py:587
  8.3 5.8 %pack_values.1 = (bf16[4,6,128,128]{3,2,1,0:T(8,128)(2,1)}, bf16[4,6,128,128]{3,2,1,0:T(8,128)(2,1)}, bf16[4,6,128,128]{3,2,1,0:T(8,128)(2,1)}, bf16[4,48,128,128]{3,2,1,0:T(8,128)(2,1)}) custom-call(s32[4,32]{1,0:T(4,128)} %bitcast.35, bf16[4,32,128,128]{3,2,1,0:T(8,128)(2,1)} %bitcast.32), custom_call_target="tpu_custom_call" | custom-call | tf_op jit(solution)/shard_map/pack_values/pallas_call | solution.py:411
  14.1 1.2 collective-permute-start.5
  15.5 0.3 select_reduce_fusion.3
  15.8 12.5 %collective-permute-done.refs_3_ = bf16[16,128,128]{2,1,0:T(8,128)(2,1)S(1)} collective-permute-done((bf16[16,128,128]{2,1,0:T(8,128)(2,1)}, bf16[16,128,128]{2,1,0:T(8,128)(2,1)S(1)}, u32[]{:S(2)}, u32[]{:S(2)}) %collective-permute-start) | collective-permute-done | bytes 524320 | tf_op jit(solution)/shard_map/ppermute | solution.py:587
  28.3 0.6 collective-permute-start.8
  28.9 25.0 %collective-permute-done.2.refs_5_ = bf16[16,128,128]{2,1,0:T(8,128)(2,1)S(1)} collective-permute-done((bf16[16,128,128]{2,1,0:T(8,128)(2,1)}, bf16[16,128,128]{2,1,0:T(8,128)(2,1)S(1)}, u32[]{:S(2)}, u32[]{:S(2)}) %collective-permute-start.2) | collective-permute-done | bytes 524320 | tf_op jit(solution)/shard_map/ppermute | solution.py:587
  53.9 1.2 collective-permute-start.10
  55.2 0.8 maximum_select_fusion.refs_4_.table_ref
  56.0 12.0 %home_sweep.3.left_ref = f32[528,128]{1,0:T(8,128)} custom-call(f32[4]{0:T(128)} %temp_ref.5, bf16[2048,128]{1,0:T(8,128)(2,1)} %bitcast.29, bf16[2048,128]{1,0:T(8,128)(2,1)} %bitcast.20, bf16[2048,128]{1,0:T(8,128)(2,1)} %bitcast.23, bf16[2048,128]{1,0:T(8,128)(2,1)} %bitcast.26, f32[512,128]{1,0:T(8,128)} %maximum_select_fusion.refs_4_.table_ref), custom_call_target="tpu_custom_call" | custom-call | tf_op jit(solution)/shard_map/home_sweep/pallas_call | solution.py:544
  68.0 0.3 collective-permute-start.4
  68.3 6.1 %pack_keys.1 = (bf16[2,6,128,128]{3,2,1,0:T(8,128)(2,1)}, bf16[1,6,128,128]{3,2,1,0:T(8,128)(2,1)}, bf16[2,6,128,128]{3,2,1,0:T(8,128)(2,1)}, bf16[2,6,128,128]{3,2,1,0:T(8,128)(2,1)}, bf16[4,48,128,128]{3,2,1,0:T(8,128)(2,1)}) custom-call(s32[4,32]{1,0:T(4,128)} %bitcast.36, f32[4,32,128,128]{3,2,1,0:T(8,128)} %bitcast.19), custom_call_target="tpu_custom_call" | custom-call | tf_op jit(solution)/shard_map/pack_keys/pallas_call | solution.py:411
  74.5 0.3 dynamic_update_slice.92
  75.1 3.1 %collective-permute-done.6.refs_1_ = s32[4,32]{1,0:T(4,128)S(1)} collective-permute-done((s32[4,32]{1,0:T(4,128)S(1)}, s32[4,32]{1,0:T(4,128)S(1)}, u32[]{:S(2)}, u32[]{:S(2)}) %collective-permute-start.6) | collective-permute-done | bytes 544 | tf_op jit(solution)/shard_map/ppermute | solution.py:587
  78.2 1.3 collective-permute-start.7
  79.5 0.3 select_reduce_fusion.2
  79.9 2.0 home_renew.3.refs_4_.table_ref
  81.8 1.3 collective-permute-start.27
  83.2 1.3 collective-permute-start.29
  84.5 0.9 collective-permute-start.15
  85.4 3.9 %home_pages.1 = (bf16[4,48,128,128]{3,2,1,0:T(8,128)(2,1)}, bf16[12,128,128]{2,1,0:T(8,128)(2,1)}) custom-call(s32[4,32]{1,0:T(4,128)} %copy-done.10, s32[4,32]{1,0:T(4,128)} %copy-done.13, s32[4,32]{1,0:T(4,128)} %copy-done.11, bf16[16,128,128]{2,1,0:T(8,128)(2,1)} %copy-done.1, bf16[16,128,128]{2,1,0:T(8,128)(2,1)} %copy-done.2, ...), custom_call_target="tpu_custom_call", output_to_operand_aliasing={{0}: (9, {})} | custom-call | tf_op jit(solution)/shard_map/home_pages/pallas_call | solution.py:482
  89.4 12.2 %home_sweep.4.left_ref = f32[528,128]{1,0:T(8,128)} custom-call(f32[4]{0:T(128)} %temp_ref.5, bf16[2048,128]{1,0:T(8,128)(2,1)} %bitcast.30, bf16[2048,128]{1,0:T(8,128)(2,1)} %bitcast.21, bf16[2048,128]{1,0:T(8,128)(2,1)} %bitcast.24, bf16[2048,128]{1,0:T(8,128)(2,1)} %bitcast.27, f32[512,128]{1,0:T(8,128)} %home_renew.3.refs_4_.table_ref), custom_call_target="tpu_custom_call" | custom-call | tf_op jit(solution)/shard_map/home_sweep/pallas_call | solution.py:544
  101.6 2.5 %collective-permute-start.11 = (f32[528,128]{1,0:T(8,128)}, f32[528,128]{1,0:T(8,128)S(1)}, u32[]{:S(2)}, u32[]{:S(2)}) collective-permute-start(f32[528,128]{1,0:T(8,128)} %home_sweep.4.left_ref), channel_id=1, source_target_pairs={{0,1},{1,0},{2,3},{3,2},{4,5},{5,4},{6,7},{7,6},{8,9},{9,8},{10,11... | collective-permute-start | bytes 811016 | tf_op jit(solution)/shard_map/ppermute | solution.py:584
  104.0 0.6 broadcast_compare_fusion.1
  104.9 0.3 select_reduce_fusion.1
  105.4 0.7 copy-done.7
  106.1 2.0 home_renew.4.refs_4_.table_ref
  108.1 11.9 %home_sweep.5.left_ref = f32[528,128]{1,0:T(8,128)} custom-call(f32[4]{0:T(128)} %temp_ref.5, bf16[2048,128]{1,0:T(8,128)(2,1)} %bitcast.31, bf16[2048,128]{1,0:T(8,128)(2,1)} %bitcast.22, bf16[2048,128]{1,0:T(8,128)(2,1)} %bitcast.25, bf16[2048,128]{1,0:T(8,128)(2,1)} %bitcast.28, f32[512,128]{1,0:T(8,128)} %home_renew.4.refs_4_.table_ref), custom_call_target="tpu_custom_call" | custom-call | tf_op jit(solution)/shard_map/home_sweep/pallas_call | solution.py:544
  120.0 0.4 collective-permute-start.12
  120.6 0.3 select_reduce_fusion
  121.8 0.7 collective-permute-start.19
  122.5 2.0 home_renew.5
  124.5 1.6 collective-permute-start.21
  126.2 0.9 constant_dynamic-update-slice_fusion.15
  127.1 12.4 %collective-permute-done.15 = bf16[2,6,128,128]{3,2,1,0:T(8,128)(2,1)} collective-permute-done((bf16[2,6,128,128]{3,2,1,0:T(8,128)(2,1)}, bf16[2,6,128,128]{3,2,1,0:T(8,128)(2,1)}, u32[]{:S(2)}, u32[]{:S(2)}) %collective-permute-start.15) | collective-permute-done | bytes 393248 | tf_op jit(solution)/shard_map/ppermute | solution.py:587
  139.5 1.1 collective-permute-start.13
  140.7 1.0 constant_dynamic-update-slice_fusion.5
  141.7 29.9 %collective-permute-done.13 = f32[256,128]{1,0:T(8,128)S(1)} collective-permute-done((f32[256,128]{1,0:T(8,128)S(1)}, f32[256,128]{1,0:T(8,128)S(1)}, u32[]{:S(2)}, u32[]{:S(2)}) %collective-permute-start.13) | collective-permute-done | bytes 131104 | tf_op jit(solution)/shard_map/ppermute | solution.py:587
  171.6 3.2 %collective-permute-start.17 = (bf16[1,6,128,128]{3,2,1,0:T(8,128)(2,1)S(1)}, bf16[1,6,128,128]{3,2,1,0:T(8,128)(2,1)S(1)}, u32[]{:S(2)}, u32[]{:S(2)}) collective-permute-start(bf16[1,6,128,128]{3,2,1,0:T(8,128)(2,1)S(1)} %copy-done.16), channel_id=1, source_target_pairs={{0,4},{4,0},{8,12},{12,8},{1,5},{5,1},{9,13},{13,9},{2,6},{6,2},{1... | collective-permute-start | bytes 589832 | tf_op jit(solution)/shard_map/ppermute | solution.py:587
  174.9 1.8 constant_dynamic-update-slice_fusion.13
  176.7 3.0 %collective-permute-start.26 = (bf16[4,6,128,128]{3,2,1,0:T(8,128)(2,1)S(1)}, bf16[4,6,128,128]{3,2,1,0:T(8,128)(2,1)S(1)}, u32[]{:S(2)}, u32[]{:S(2)}) collective-permute-start(bf16[4,6,128,128]{3,2,1,0:T(8,128)(2,1)S(1)} %collective-permute-done.25), channel_id=1, source_target_pairs={{0,1},{1,0},{2,3},{3,2},{4,5},{5,4},{6,7},{7,6},{8,9},{9,8},{10,11... | collective-permute-start | bytes 2359304 | tf_op jit(solution)/shard_map/ppermute | solution.py:584
  179.7 3.7 %collective-permute-start.16 = (bf16[2,6,128,128]{3,2,1,0:T(8,128)(2,1)}, bf16[2,6,128,128]{3,2,1,0:T(8,128)(2,1)S(1)}, u32[]{:S(2)}, u32[]{:S(2)}) collective-permute-start(bf16[2,6,128,128]{3,2,1,0:T(8,128)(2,1)} %collective-permute-done.15), channel_id=1, source_target_pairs={{0,1},{1,0},{2,3},{3,2},{4,5},{5,4},{6,7},{7,6},{8,9},{9,8},{10,11... | collective-permute-start | bytes 1179656 | tf_op jit(solution)/shard_map/ppermute | solution.py:584
  183.5 0.5 collective-permute-start.18
  184.0 2.3 %collective-permute-start.20 = (bf16[2,6,128,128]{3,2,1,0:T(8,128)(2,1)S(1)}, bf16[2,6,128,128]{3,2,1,0:T(8,128)(2,1)S(1)}, u32[]{:S(2)}, u32[]{:S(2)}) collective-permute-start(bf16[2,6,128,128]{3,2,1,0:T(8,128)(2,1)S(1)} %collective-permute-done.19), channel_id=1, source_target_pairs={{0,1},{1,0},{2,3},{3,2},{4,5},{5,4},{6,7},{7,6},{8,9},{9,8},{10,11... | collective-permute-start | bytes 1179656 | tf_op jit(solution)/shard_map/ppermute | solution.py:584
  186.6 0.8 constant_dynamic-update-slice_fusion.12
  187.4 0.7 constant_dynamic-update-slice_fusion.11
  188.1 0.3 collective-permute-start.22
  188.4 0.7 constant_dynamic-update-slice_fusion.10
  189.0 0.8 constant_dynamic-update-slice_fusion.9
  189.9 15.8 %collective-permute-done.23 = bf16[2,6,128,128]{3,2,1,0:T(8,128)(2,1)S(1)} collective-permute-done((bf16[2,6,128,128]{3,2,1,0:T(8,128)(2,1)}, bf16[2,6,128,128]{3,2,1,0:T(8,128)(2,1)S(1)}, u32[]{:S(2)}, u32[]{:S(2)}) %collective-permute-start.23) | collective-permute-done | bytes 393248 | tf_op jit(solution)/shard_map/ppermute | solution.py:587
  205.7 0.9 collective-permute-start.30
  206.6 0.8 constant_dynamic-update-slice_fusion.8
  207.4 0.8 bitcast_dynamic-update-slice_fusion.1
  208.2 0.8 bitcast_dynamic-update-slice_fusion
  208.9 0.8 constant_dynamic-update-slice_fusion.7
  209.8 1.1 constant_dynamic-update-slice_fusion.4
  210.8 2.2 %constant_dynamic-update-slice_fusion.3 = bf16[4,48,128,128]{3,2,1,0:T(8,128)(2,1)} fusion(bf16[4,48,128,128]{3,2,1,0:T(8,128)(2,1)} %constant_dynamic-update-slice_fusion.4, bf16[4,6,128,128]{3,2,1,0:T(8,128)(2,1)} %collective-permute-done.27, s32[]{:T(128)S(6)} %select_n.109), kind=kLoop, calls=%fused_computation.22 | loop fusion | bytes 1572868 | tf_op jit(solution)/shard_map/dynamic_update_slice | solution.py:626
  213.0 1.1 constant_dynamic-update-slice_fusion.2
  214.1 2.2 %constant_dynamic-update-slice_fusion.1 = bf16[4,48,128,128]{3,2,1,0:T(8,128)(2,1)} fusion(bf16[4,48,128,128]{3,2,1,0:T(8,128)(2,1)} %constant_dynamic-update-slice_fusion.2, bf16[4,6,128,128]{3,2,1,0:T(8,128)(2,1)} %collective-permute-done.29, s32[]{:T(128)S(6)} %select_n.114), kind=kLoop, calls=%fused_computation.20 | loop fusion | bytes 1572868 | tf_op jit(solution)/shard_map/dynamic_update_slice | solution.py:626
  216.3 1.1 constant_dynamic-update-slice_fusion
  217.4 0.8 constant_dynamic-update-slice_fusion.6
  (95 shorter events, 3.1 us)
Async XLA Ops:
  0.6 1.0 copy-start
  1.7 53.5 %collective-permute-start.3 = (f32[256,128]{1,0:T(8,128)S(1)}, f32[256,128]{1,0:T(8,128)S(1)}, u32[]{:S(2)}, u32[]{:S(2)}) collective-permute-start(f32[256,128]{1,0:T(8,128)S(1)} %dynamic-slice_bitcast_fusion), channel_id=1, source_target_pairs={{0,1},{1,0},{2,3},{3,2},{4,5},{5,4},{6,7},{7,6},{8,9},{9,8},{10,11... | collective-permute-start | bytes 393224 | tf_op jit(solution)/shard_map/ppermute | solution.py:584
  2.4 11.6 %copy-start.8 = (s32[4,32,1]{1,2,0:T(1,128)S(1)}, s32[4,32,1]{1,2,0:T(1,128)}, u32[]{:S(2)}) copy-start(s32[4,32,1]{1,2,0:T(1,128)} %param.9) | copy-start | bytes 1540
  5.6 22.7 %collective-permute-start = (bf16[16,128,128]{2,1,0:T(8,128)(2,1)}, bf16[16,128,128]{2,1,0:T(8,128)(2,1)S(1)}, u32[]{:S(2)}, u32[]{:S(2)}) collective-permute-start(bf16[16,128,128]{2,1,0:T(8,128)(2,1)} %get-tuple-element.34), channel_id=1, source_target_pairs={{0,4},{4,0},{8,12},{12,8},{1,5},{5,1},{9,13},{13,9},{2,6},{6,2},{1... | collective-permute-start | bytes 1572872 | tf_op jit(solution)/shard_map/ppermute | solution.py:587
  5.6 49.5 %collective-permute-start.1 = (bf16[16,128,128]{2,1,0:T(8,128)(2,1)}, bf16[16,128,128]{2,1,0:T(8,128)(2,1)S(1)}, u32[]{:S(2)}, u32[]{:S(2)}) collective-permute-start(bf16[16,128,128]{2,1,0:T(8,128)(2,1)} %get-tuple-element.35), channel_id=1, source_target_pairs={{0,8},{4,12},{8,0},{12,4},{1,9},{5,13},{9,1},{13,5},{2,10},{6,14},... | collective-permute-start | bytes 1572872 | tf_op jit(solution)/shard_map/ppermute | solution.py:587
  8.1 45.8 %collective-permute-start.2 = (bf16[16,128,128]{2,1,0:T(8,128)(2,1)}, bf16[16,128,128]{2,1,0:T(8,128)(2,1)S(1)}, u32[]{:S(2)}, u32[]{:S(2)}) collective-permute-start(bf16[16,128,128]{2,1,0:T(8,128)(2,1)} %get-tuple-element.36), channel_id=1, source_target_pairs={{0,12},{4,8},{8,4},{12,0},{1,13},{5,9},{9,5},{13,1},{2,14},{6,10},... | collective-permute-start | bytes 1572872 | tf_op jit(solution)/shard_map/ppermute | solution.py:587
  14.1 60.7 %copy-start.9 = (s32[4,32,1]{1,2,0:T(1,128)S(1)}, s32[4,32,1]{1,2,0:T(1,128)}, u32[]{:S(2)}) copy-start(s32[4,32,1]{1,2,0:T(1,128)} %param.9) | copy-start | bytes 1540
  14.1 60.7 %collective-permute-start.5 = (s32[4,32]{1,0:T(4,128)S(1)}, s32[4,32]{1,0:T(4,128)S(1)}, u32[]{:S(2)}, u32[]{:S(2)}) collective-permute-start(s32[4,32]{1,0:T(4,128)S(1)} %bitcast.37), channel_id=1, source_target_pairs={{0,4},{4,0},{8,12},{12,8},{1,5},{5,1},{9,13},{13,9},{2,6},{6,2},{1... | collective-permute-start | bytes 1544 | tf_op jit(solution)/shard_map/ppermute | solution.py:587
  28.3 27.8 %copy-start.1 = (bf16[16,128,128]{2,1,0:T(8,128)(2,1)}, bf16[16,128,128]{2,1,0:T(8,128)(2,1)S(1)}, u32[]{:S(2)}) copy-start(bf16[16,128,128]{2,1,0:T(8,128)(2,1)S(1)} %collective-permute-done.refs_3_) | copy-start | bytes 1572868
  28.3 54.9 %collective-permute-start.8 = (bf16[16,128,128]{2,1,0:T(8,128)(2,1)S(1)}, bf16[16,128,128]{2,1,0:T(8,128)(2,1)S(1)}, u32[]{:S(2)}, u32[]{:S(2)}) collective-permute-start(bf16[16,128,128]{2,1,0:T(8,128)(2,1)S(1)} %collective-permute-done.refs_3_), channel_id=1, source_target_pairs={{0,1},{1,0},{2,3},{3,2},{4,5},{5,4},{6,7},{7,6},{8,9},{9,8},{10,11... | collective-permute-start | bytes 1572872 | tf_op jit(solution)/shard_map/ppermute | solution.py:584
  53.9 2.1 copy-start.3
  53.9 30.6 %collective-permute-start.10 = (bf16[16,128,128]{2,1,0:T(8,128)(2,1)S(1)}, bf16[16,128,128]{2,1,0:T(8,128)(2,1)}, u32[]{:S(2)}, u32[]{:S(2)}) collective-permute-start(bf16[16,128,128]{2,1,0:T(8,128)(2,1)S(1)} %collective-permute-done.2.refs_5_), channel_id=1, source_target_pairs={{0,1},{1,0},{2,3},{3,2},{4,5},{5,4},{6,7},{7,6},{8,9},{9,8},{10,11... | collective-permute-start | bytes 1572872 | tf_op jit(solution)/shard_map/ppermute | solution.py:584
  55.1 0.9 copy-start.2
  55.1 30.3 %collective-permute-start.9 = (bf16[16,128,128]{2,1,0:T(8,128)(2,1)S(1)}, bf16[16,128,128]{2,1,0:T(8,128)(2,1)}, u32[]{:S(2)}, u32[]{:S(2)}) collective-permute-start(bf16[16,128,128]{2,1,0:T(8,128)(2,1)S(1)} %collective-permute-done.1.refs_4_), channel_id=1, source_target_pairs={{0,1},{1,0},{2,3},{3,2},{4,5},{5,4},{6,7},{7,6},{8,9},{9,8},{10,11... | collective-permute-start | bytes 1572872 | tf_op jit(solution)/shard_map/ppermute | solution.py:584
  68.0 11.5 %collective-permute-start.4 = (f32[528,128]{1,0:T(8,128)}, f32[528,128]{1,0:T(8,128)}, u32[]{:S(2)}, u32[]{:S(2)}) collective-permute-start(f32[528,128]{1,0:T(8,128)} %home_sweep.3.left_ref), channel_id=1, source_target_pairs={{0,1},{1,0},{2,3},{3,2},{4,5},{5,4},{6,7},{7,6},{8,9},{9,8},{10,11... | collective-permute-start | bytes 811016 | tf_op jit(solution)/shard_map/ppermute | solution.py:584
  74.8 10.6 %copy-start.10 = (s32[4,32]{1,0:T(4,128)}, s32[4,32]{1,0:T(4,128)S(1)}, u32[]{:S(2)}) copy-start(s32[4,32]{1,0:T(4,128)S(1)} %collective-permute-done.5.refs_0_) | copy-start | bytes 1540
  74.8 3.4 %collective-permute-start.6 = (s32[4,32]{1,0:T(4,128)S(1)}, s32[4,32]{1,0:T(4,128)S(1)}, u32[]{:S(2)}, u32[]{:S(2)}) collective-permute-start(s32[4,32]{1,0:T(4,128)S(1)} %bitcast.39), channel_id=1, source_target_pairs={{0,8},{4,12},{8,0},{12,4},{1,9},{5,13},{9,1},{13,5},{2,10},{6,14},... | collective-permute-start | bytes 1544 | tf_op jit(solution)/shard_map/ppermute | solution.py:587
  78.2 7.2 %copy-start.13 = (s32[4,32]{1,0:T(4,128)}, s32[4,32]{1,0:T(4,128)S(1)}, u32[]{:S(2)}) copy-start(s32[4,32]{1,0:T(4,128)S(1)} %collective-permute-done.6.refs_1_) | copy-start | bytes 1540
  78.2 3.6 %collective-permute-start.7 = (s32[4,32]{1,0:T(4,128)S(1)}, s32[4,32]{1,0:T(4,128)S(1)}, u32[]{:S(2)}, u32[]{:S(2)}) collective-permute-start(s32[4,32]{1,0:T(4,128)S(1)} %bitcast.40), channel_id=1, source_target_pairs={{0,12},{4,8},{8,4},{12,0},{1,13},{5,9},{9,5},{13,1},{2,14},{6,10},... | collective-permute-start | bytes 1544 | tf_op jit(solution)/shard_map/ppermute | solution.py:587
  79.5 45.0 %collective-permute-start.25 = (bf16[4,6,128,128]{3,2,1,0:T(8,128)(2,1)}, bf16[4,6,128,128]{3,2,1,0:T(8,128)(2,1)S(1)}, u32[]{:S(2)}, u32[]{:S(2)}) collective-permute-start(bf16[4,6,128,128]{3,2,1,0:T(8,128)(2,1)} %get-tuple-element.39), channel_id=1, source_target_pairs={{0,4},{4,0},{8,12},{12,8},{1,5},{5,1},{9,13},{13,9},{2,6},{6,2},{1... | collective-permute-start | bytes 2359304 | tf_op jit(solution)/shard_map/ppermute | solution.py:587
  81.8 3.6 %copy-start.11 = (s32[4,32]{1,0:T(4,128)}, s32[4,32]{1,0:T(4,128)S(1)}, u32[]{:S(2)}) copy-start(s32[4,32]{1,0:T(4,128)S(1)} %collective-permute-done.7.refs_2_) | copy-start | bytes 1540
  81.8 93.0 %collective-permute-start.27 = (bf16[4,6,128,128]{3,2,1,0:T(8,128)(2,1)}, bf16[4,6,128,128]{3,2,1,0:T(8,128)(2,1)}, u32[]{:S(2)}, u32[]{:S(2)}) collective-permute-start(bf16[4,6,128,128]{3,2,1,0:T(8,128)(2,1)} %get-tuple-element.58), channel_id=1, source_target_pairs={{0,8},{4,12},{8,0},{12,4},{1,9},{5,13},{9,1},{13,5},{2,10},{6,14},... | collective-permute-start | bytes 2359304 | tf_op jit(solution)/shard_map/ppermute | solution.py:587
  83.2 2.2 %copy-start.4 = (bf16[16,128,128]{2,1,0:T(8,128)(2,1)}, bf16[16,128,128]{2,1,0:T(8,128)(2,1)S(1)}, u32[]{:S(2)}) copy-start(bf16[16,128,128]{2,1,0:T(8,128)(2,1)S(1)} %collective-permute-done.8.refs_6_) | copy-start | bytes 1572868
  83.2 93.5 %collective-permute-start.29 = (bf16[4,6,128,128]{3,2,1,0:T(8,128)(2,1)}, bf16[4,6,128,128]{3,2,1,0:T(8,128)(2,1)}, u32[]{:S(2)}, u32[]{:S(2)}) collective-permute-start(bf16[4,6,128,128]{3,2,1,0:T(8,128)(2,1)} %get-tuple-element.60), channel_id=1, source_target_pairs={{0,12},{4,8},{8,4},{12,0},{1,13},{5,9},{9,5},{13,1},{2,14},{6,10},... | collective-permute-start | bytes 2359304 | tf_op jit(solution)/shard_map/ppermute | solution.py:587
  84.5 55.0 %collective-permute-start.15 = (bf16[2,6,128,128]{3,2,1,0:T(8,128)(2,1)}, bf16[2,6,128,128]{3,2,1,0:T(8,128)(2,1)}, u32[]{:S(2)}, u32[]{:S(2)}) collective-permute-start(bf16[2,6,128,128]{3,2,1,0:T(8,128)(2,1)} %get-tuple-element.46), channel_id=1, source_target_pairs={{0,4},{4,0},{8,12},{12,8},{1,5},{5,1},{9,13},{13,9},{2,6},{6,2},{1... | collective-permute-start | bytes 1179656 | tf_op jit(solution)/shard_map/ppermute | solution.py:587
  85.4 36.4 %copy-start.15 = (bf16[2,6,128,128]{3,2,1,0:T(8,128)(2,1)S(1)}, bf16[2,6,128,128]{3,2,1,0:T(8,128)(2,1)}, u32[]{:S(2)}) copy-start(bf16[2,6,128,128]{3,2,1,0:T(8,128)(2,1)} %get-tuple-element.50) | copy-start | bytes 1179652
  89.4 31.0 %copy-start.12 = (s32[4,32]{1,0:T(4,128)S(1)}, s32[4,32]{1,0:T(4,128)}, u32[]{:S(2)}) copy-start(s32[4,32]{1,0:T(4,128)} %copy-done.11) | copy-start | bytes 1540
  89.4 82.2 %copy-start.16 = (bf16[1,6,128,128]{3,2,1,0:T(8,128)(2,1)S(1)}, bf16[1,6,128,128]{3,2,1,0:T(8,128)(2,1)}, u32[]{:S(2)}) copy-start(bf16[1,6,128,128]{3,2,1,0:T(8,128)(2,1)} %get-tuple-element.48) | copy-start | bytes 589828
  101.6 3.8 %collective-permute-start.11 = (f32[528,128]{1,0:T(8,128)}, f32[528,128]{1,0:T(8,128)S(1)}, u32[]{:S(2)}, u32[]{:S(2)}) collective-permute-start(f32[528,128]{1,0:T(8,128)} %home_sweep.4.left_ref), channel_id=1, source_target_pairs={{0,1},{1,0},{2,3},{3,2},{4,5},{5,4},{6,7},{7,6},{8,9},{9,8},{10,11... | collective-permute-start | bytes 811016 | tf_op jit(solution)/shard_map/ppermute | solution.py:584
  105.4 0.7 copy-start.7
  120.0 1.8 collective-permute-start.12
  121.6 96.7 %copy-start.14 = (s32[4,48]{1,0:T(4,128)}, s32[4,48]{1,0:T(4,128)S(1)}, u32[]{:S(2)}) copy-start(s32[4,48]{1,0:T(4,128)S(1)} %dynamic_update_slice.95) | copy-start | bytes 2308
  121.8 0.7 copy-start.6
  121.8 61.7 %collective-permute-start.19 = (bf16[2,6,128,128]{3,2,1,0:T(8,128)(2,1)S(1)}, bf16[2,6,128,128]{3,2,1,0:T(8,128)(2,1)S(1)}, u32[]{:S(2)}, u32[]{:S(2)}) collective-permute-start(bf16[2,6,128,128]{3,2,1,0:T(8,128)(2,1)S(1)} %copy-done.15), channel_id=1, source_target_pairs={{0,8},{4,12},{8,0},{12,4},{1,9},{5,13},{9,1},{13,5},{2,10},{6,14},... | collective-permute-start | bytes 1179656 | tf_op jit(solution)/shard_map/ppermute | solution.py:587
  124.5 59.0 %collective-permute-start.21 = (bf16[12,128,128]{2,1,0:T(8,128)(2,1)}, bf16[12,128,128]{2,1,0:T(8,128)(2,1)S(1)}, u32[]{:S(2)}, u32[]{:S(2)}) collective-permute-start(bf16[12,128,128]{2,1,0:T(8,128)(2,1)} %get-tuple-element.43), channel_id=1, source_target_pairs={{0,4},{4,0},{8,12},{12,8},{1,5},{5,1},{9,13},{13,9},{2,6},{6,2},{1... | collective-permute-start | bytes 1179656 | tf_op jit(solution)/shard_map/ppermute | solution.py:587
  139.5 32.0 %collective-permute-start.13 = (f32[256,128]{1,0:T(8,128)S(1)}, f32[256,128]{1,0:T(8,128)S(1)}, u32[]{:S(2)}, u32[]{:S(2)}) collective-permute-start(f32[256,128]{1,0:T(8,128)S(1)} %get-tuple-element.71), channel_id=1, source_target_pairs={{0,8},{4,12},{8,0},{12,4},{1,9},{5,13},{9,1},{13,5},{2,10},{6,14},... | collective-permute-start | bytes 393224 | tf_op jit(solution)/shard_map/ppermute | solution.py:587
  171.6 8.1 %collective-permute-start.17 = (bf16[1,6,128,128]{3,2,1,0:T(8,128)(2,1)S(1)}, bf16[1,6,128,128]{3,2,1,0:T(8,128)(2,1)S(1)}, u32[]{:S(2)}, u32[]{:S(2)}) collective-permute-start(bf16[1,6,128,128]{3,2,1,0:T(8,128)(2,1)S(1)} %copy-done.16), channel_id=1, source_target_pairs={{0,4},{4,0},{8,12},{12,8},{1,5},{5,1},{9,13},{13,9},{2,6},{6,2},{1... | collective-permute-start | bytes 589832 | tf_op jit(solution)/shard_map/ppermute | solution.py:587
  174.8 9.2 %collective-permute-start.14 = (f32[2,256,128]{2,1,0:T(8,128)S(1)}, f32[2,256,128]{2,1,0:T(8,128)S(1)}, u32[]{:S(2)}, u32[]{:S(2)}) collective-permute-start(f32[2,256,128]{2,1,0:T(8,128)S(1)} %pad_maximum_fusion), channel_id=1, source_target_pairs={{0,4},{4,0},{8,12},{12,8},{1,5},{5,1},{9,13},{13,9},{2,6},{6,2},{1... | collective-permute-start | bytes 786440 | tf_op jit(solution)/shard_map/ppermute | solution.py:587
  176.7 33.0 %collective-permute-start.26 = (bf16[4,6,128,128]{3,2,1,0:T(8,128)(2,1)S(1)}, bf16[4,6,128,128]{3,2,1,0:T(8,128)(2,1)S(1)}, u32[]{:S(2)}, u32[]{:S(2)}) collective-permute-start(bf16[4,6,128,128]{3,2,1,0:T(8,128)(2,1)S(1)} %collective-permute-done.25), channel_id=1, source_target_pairs={{0,1},{1,0},{2,3},{3,2},{4,5},{5,4},{6,7},{7,6},{8,9},{9,8},{10,11... | collective-permute-start | bytes 2359304 | tf_op jit(solution)/shard_map/ppermute | solution.py:584
  179.7 6.6 %collective-permute-start.16 = (bf16[2,6,128,128]{3,2,1,0:T(8,128)(2,1)}, bf16[2,6,128,128]{3,2,1,0:T(8,128)(2,1)S(1)}, u32[]{:S(2)}, u32[]{:S(2)}) collective-permute-start(bf16[2,6,128,128]{3,2,1,0:T(8,128)(2,1)} %collective-permute-done.15), channel_id=1, source_target_pairs={{0,1},{1,0},{2,3},{3,2},{4,5},{5,4},{6,7},{7,6},{8,9},{9,8},{10,11... | collective-permute-start | bytes 1179656 | tf_op jit(solution)/shard_map/ppermute | solution.py:584
  183.5 29.6 %collective-permute-start.28 = (bf16[4,6,128,128]{3,2,1,0:T(8,128)(2,1)}, bf16[4,6,128,128]{3,2,1,0:T(8,128)(2,1)S(1)}, u32[]{:S(2)}, u32[]{:S(2)}) collective-permute-start(bf16[4,6,128,128]{3,2,1,0:T(8,128)(2,1)} %collective-permute-done.27), channel_id=1, source_target_pairs={{0,1},{1,0},{2,3},{3,2},{4,5},{5,4},{6,7},{7,6},{8,9},{9,8},{10,11... | collective-permute-start | bytes 2359304 | tf_op jit(solution)/shard_map/ppermute | solution.py:584
  183.5 4.6 %collective-permute-start.18 = (bf16[1,6,128,128]{3,2,1,0:T(8,128)(2,1)S(1)}, bf16[1,6,128,128]{3,2,1,0:T(8,128)(2,1)S(1)}, u32[]{:S(2)}, u32[]{:S(2)}) collective-permute-start(bf16[1,6,128,128]{3,2,1,0:T(8,128)(2,1)S(1)} %collective-permute-done.17), channel_id=1, source_target_pairs={{0,1},{1,0},{2,3},{3,2},{4,5},{5,4},{6,7},{7,6},{8,9},{9,8},{10,11... | collective-permute-start | bytes 589832 | tf_op jit(solution)/shard_map/ppermute | solution.py:584
  184.0 22.6 %collective-permute-start.20 = (bf16[2,6,128,128]{3,2,1,0:T(8,128)(2,1)S(1)}, bf16[2,6,128,128]{3,2,1,0:T(8,128)(2,1)S(1)}, u32[]{:S(2)}, u32[]{:S(2)}) collective-permute-start(bf16[2,6,128,128]{3,2,1,0:T(8,128)(2,1)S(1)} %collective-permute-done.19), channel_id=1, source_target_pairs={{0,1},{1,0},{2,3},{3,2},{4,5},{5,4},{6,7},{7,6},{8,9},{9,8},{10,11... | collective-permute-start | bytes 1179656 | tf_op jit(solution)/shard_map/ppermute | solution.py:584
  186.3 31.1 %copy-start.5 = (f32[4,256,128]{2,1,0:T(8,128)}, f32[4,256,128]{2,1,0:T(8,128)S(1)}, u32[]{:S(2)}) copy-start(f32[4,256,128]{2,1,0:T(8,128)S(1)} %slice_dynamic-update-slice_fusion) | copy-start | bytes 1572868
  186.3 19.4 %collective-permute-start.23 = (bf16[2,6,128,128]{3,2,1,0:T(8,128)(2,1)}, bf16[2,6,128,128]{3,2,1,0:T(8,128)(2,1)S(1)}, u32[]{:S(2)}, u32[]{:S(2)}) collective-permute-start(bf16[2,6,128,128]{3,2,1,0:T(8,128)(2,1)} %get-tuple-element.54), channel_id=1, source_target_pairs={{0,12},{4,8},{8,4},{12,0},{1,13},{5,9},{9,5},{13,1},{2,14},{6,10},... | collective-permute-start | bytes 1179656 | tf_op jit(solution)/shard_map/ppermute | solution.py:587
  188.1 20.1 %collective-permute-start.22 = (bf16[12,128,128]{2,1,0:T(8,128)(2,1)S(1)}, bf16[12,128,128]{2,1,0:T(8,128)(2,1)S(1)}, u32[]{:S(2)}, u32[]{:S(2)}) collective-permute-start(bf16[12,128,128]{2,1,0:T(8,128)(2,1)S(1)} %collective-permute-done.21), channel_id=1, source_target_pairs={{0,1},{1,0},{2,3},{3,2},{4,5},{5,4},{6,7},{7,6},{8,9},{9,8},{10,11... | collective-permute-start | bytes 1179656 | tf_op jit(solution)/shard_map/ppermute | solution.py:584
  205.7 10.6 %collective-permute-start.30 = (bf16[4,6,128,128]{3,2,1,0:T(8,128)(2,1)}, bf16[4,6,128,128]{3,2,1,0:T(8,128)(2,1)S(1)}, u32[]{:S(2)}, u32[]{:S(2)}) collective-permute-start(bf16[4,6,128,128]{3,2,1,0:T(8,128)(2,1)} %collective-permute-done.29), channel_id=1, source_target_pairs={{0,1},{1,0},{2,3},{3,2},{4,5},{5,4},{6,7},{7,6},{8,9},{9,8},{10,11... | collective-permute-start | bytes 2359304 | tf_op jit(solution)/shard_map/ppermute | solution.py:584
  206.6 10.9 %collective-permute-start.24 = (bf16[2,6,128,128]{3,2,1,0:T(8,128)(2,1)S(1)}, bf16[2,6,128,128]{3,2,1,0:T(8,128)(2,1)S(1)}, u32[]{:S(2)}, u32[]{:S(2)}) collective-permute-start(bf16[2,6,128,128]{3,2,1,0:T(8,128)(2,1)S(1)} %collective-permute-done.23), channel_id=1, source_target_pairs={{0,1},{1,0},{2,3},{3,2},{4,5},{5,4},{6,7},{7,6},{8,9},{9,8},{10,11... | collective-permute-start | bytes 1179656 | tf_op jit(solution)/shard_map/ppermute | solution.py:584
where the time goes:
time: 219 us; the launch traced here: 218 us
  waiting for transfers between devices  99.2 us (45%)
  Pallas kernels  60.8 us (28%)
  starting transfers between devices  32.2 us (15%)
  local copies, waits for them, and re-layouts  21.5 us (10%)
  other arithmetic  3.5 us (2%)
    ppermute x16, waiting for transfers between devices, facing(): return lax.ppermute(value, 'seq', [(i, i ^ bit) for i in range(ranks)])  98.8 us
    pallas_call x3, Pallas kernels, home_sweep(): pl.pallas_call(functools.partial(home_sweep_kernel, tile), out_shape=jax....  36.1 us
    dynamic_update_slice x16, local copies, waits for them, and re-layouts, place(): return lax.dynamic_update_slice(whole, part, (head, slot, 0, 0))  17.5 us
    ppermute x15, starting transfers between devices, across(): return lax.ppermute(value, 'sub', [(0, 1), (1, 0)])  16.4 us
    ppermute x16, starting transfers between devices, facing(): return lax.ppermute(value, 'seq', [(i, i ^ bit) for i in range(ranks)])  15.8 us
    pallas_call x2, Pallas kernels, pack_pages(): pl.pallas_call(functools.partial(pack_kernel, plan, capacity, with_cast),...  11.8 us
    pallas_call x3, Pallas kernels, home_renew(): pl.pallas_call(home_renew_kernel, out_shape=jax.ShapeDtypeStruct(table.sh...  5.89 us
  transfers between devices with their start and end apart: 31, of which 8 were waited for; matrix products, arithmetic and copies ran while one was open for 10% of the time, Pallas kernels for 28%

commit v1 on v0

--- a/solution.py
+++ b/solution.py
@@ -280,7 +280,7 @@
     part = cache_ref.shape[1] // cores
     first = lax.axis_index("sub") * part
     me = lax.axis_index("seq")
-    order = list(range(1, ranks)) + [0]
+    order = [2, 1, 3, 0]
     for bit in order:
         pltpu.make_async_copy(
             cache_ref.at[me ^ bit, pl.ds(first, part)], wide_ref.at[bit], in_sem.at[bit]
@@ -570,6 +570,46 @@
     )(left, right, table)
 
 
+def ids_kernel(capacity, *refs):
+    owner_refs, out_ref = refs[:-1], refs[-1]
+    heads, pages = owner_refs[0].shape
+    me = lax.axis_index("seq")
+
+    def one_head(head, carry):
+        def clear(slot, carry):
+            out_ref[head, slot] = -1
+            return carry
+
+        lax.fori_loop(0, out_ref.shape[1], clear, 0, unroll=4)
+        for bit, owner_ref in enumerate(owner_refs):
+            source = me ^ bit
+
+            def put(page, count, owner_ref=owner_ref, source=source):
+                hit = owner_ref[head, page] == me
+
+                @pl.when(hit)
+                def _():
+                    out_ref[head, source * capacity + count] = source * pages + page
+
+                return count + jnp.where(hit, 1, 0)
+
+            lax.fori_loop(0, pages, put, jnp.int32(0), unroll=4)
+        return carry
+
+    lax.fori_loop(0, heads, one_head, 0)
+
+
+def home_ids(owners, capacity):
+    smem = pl.BlockSpec(memory_space=pltpu.SMEM)
+    return pl.pallas_call(
+        functools.partial(ids_kernel, capacity),
+        out_shape=jax.ShapeDtypeStruct((owners[0].shape[0], len(owners) * capacity), jnp.int32),
+        in_specs=[smem] * len(owners),
+        out_specs=smem,
+        name="home_ids",
+    )(*owners)
+
+
 def on_home_chips(key_cache, value_cache, centroids, inv_temp, page_owner):
     heads, tokens, width = key_cache.shape
     pages = tokens // PAGE
@@ -592,13 +632,15 @@
         homed[bit] = facing(lowered[bit], bit)
 
     owner_after, value_after = tied(owner, value_cache, lowered[1])[:2]
+    owners = [owner] + [facing(owner_after, bit) for bit in range(1, ranks)]
     *value_chunks, moved_values = pack_pages(owner_after, value_after.reshape(paged), VALUE_PLAN, capacity, False)
     values_in = [facing(value_chunks[i], VALUE_PLAN[i][0]) for i in range(len(VALUE_PLAN))]
 
     owner_after, key_after = tied(owner, key_cache, value_chunks[0])[:2]
-    owners = [owner] + [facing(owner_after, bit) for bit in range(1, ranks)]
     *key_chunks, moved_keys = pack_pages(owner_after, key_after.reshape(paged), KEY_PLAN, capacity, True)
     keys_in = [facing(key_chunks[i], KEY_PLAN[i][0]) for i in range(len(KEY_PLAN) - 1)]
+
+    ids = home_ids(owners, capacity)
 
     seeds = lax.dynamic_index_in_dim(centroids, me, 0, keepdims=False)
     seeds_got = across(seeds)
@@ -644,8 +686,7 @@
     clusters = jnp.zeros(centroids.shape, centroids.dtype)
     for part, head in ((ours, me), (opposite, me ^ 2), (near[0], me ^ 1), (near[1], me ^ 3)):
         clusters = lax.dynamic_update_slice(clusters, part[None], (head, 0, 0))
-    sources = [me ^ bit for bit in range(ranks)]
-    return (clusters, moved_keys, moved_values, slot_pages(owners, sources, pages, capacity))
+    return (clusters, moved_keys, moved_values, ids)
 
 
 def slot_pages(owners, sources, pages, capacity):

time: 219 us -> 252 us (1.15)
  the two profiles are of different devices: /device:TPU:9 before, /device:TPU:0 now
where the time goes in v1:
time: 252 us; the launch traced here: 247 us
  waiting for transfers between devices  136 us (54%)
  Pallas kernels  65.9 us (26%)
  starting transfers between devices  25.9 us (10%)
  local copies, waits for them, and re-layouts  17.6 us (7%)
    ppermute x16, waiting for transfers between devices, facing(): return lax.ppermute(value, 'seq', [(i, i ^ bit) for i in range(ranks)])  135 us
    pallas_call x3, Pallas kernels, home_sweep(): pl.pallas_call(functools.partial(home_sweep_kernel, tile), out_shape=jax....  36 us
    ppermute x16, starting transfers between devices, facing(): return lax.ppermute(value, 'seq', [(i, i ^ bit) for i in range(ranks)])  23.9 us
    dynamic_update_slice x16, local copies, waits for them, and re-layouts, place(): return lax.dynamic_update_slice(whole, part, (head, slot, 0, 0))  15.1 us
    pallas_call x2, Pallas kernels, pack_pages(): pl.pallas_call(functools.partial(pack_kernel, plan, capacity, with_cast),...  11.8 us
    pallas_call x3, Pallas kernels, home_renew(): pl.pallas_call(home_renew_kernel, out_shape=jax.ShapeDtypeStruct(table.sh...  5.89 us
    pallas_call x1, Pallas kernels, home_ids(): pl.pallas_call(functools.partial(ids_kernel, capacity), out_shape=jax.Sha...  5.19 us
  transfers between devices with their start and end apart: 31, of which 11 were waited for; matrix products, arithmetic and copies ran while one was open for 6% of the time, Pallas kernels for 25%

profile of v1, /device:TPU:0, one launch (start us, length us, event | category | flops | bytes accessed | tf_op | source)
XLA Modules:
  0.0 247.3 jit_solution(3931175061417534230)
XLA Ops:
  0.6 0.0 copy-start
  0.6 0.0 copy-start.8
  0.7 3.2 %lower_keys.1 = (bf16[16,128,128]{2,1,0:T(8,128)(2,1)}, bf16[16,128,128]{2,1,0:T(8,128)(2,1)}, bf16[16,128,128]{2,1,0:T(8,128)(2,1)}, bf16[16,128,128]{2,1,0:T(8,128)(2,1)}) custom-call(f32[4,32,128,128]{3,2,1,0:T(8,128)} %bitcast.18), custom_call_target="tpu_custom_call" | custom-call | tf_op jit(solution)/shard_map/lower_keys/pallas_call | solution.py:305
  3.8 3.1 %collective-permute-start = (bf16[16,128,128]{2,1,0:T(8,128)(2,1)}, bf16[16,128,128]{2,1,0:T(8,128)(2,1)S(1)}, u32[]{:S(2)}, u32[]{:S(2)}) collective-permute-start(bf16[16,128,128]{2,1,0:T(8,128)(2,1)} %get-tuple-element.34), channel_id=1, source_target_pairs={{0,4},{4,0},{8,12},{12,8},{1,5},{5,1},{9,13},{13,9},{2,6},{6,2},{1... | collective-permute-start | bytes 1572872 | tf_op jit(solution)/shard_map/ppermute | solution.py:627
  7.0 2.5 %collective-permute-start.2 = (bf16[16,128,128]{2,1,0:T(8,128)(2,1)}, bf16[16,128,128]{2,1,0:T(8,128)(2,1)S(1)}, u32[]{:S(2)}, u32[]{:S(2)}) collective-permute-start(bf16[16,128,128]{2,1,0:T(8,128)(2,1)} %get-tuple-element.36), channel_id=1, source_target_pairs={{0,12},{4,8},{8,4},{12,0},{1,13},{5,9},{9,5},{13,1},{2,14},{6,10},... | collective-permute-start | bytes 1572872 | tf_op jit(solution)/shard_map/ppermute | solution.py:627
  9.4 0.1 collective-permute-start.1
  9.6 10.0 %collective-permute-done.refs_3_ = bf16[16,128,128]{2,1,0:T(8,128)(2,1)S(1)} collective-permute-done((bf16[16,128,128]{2,1,0:T(8,128)(2,1)}, bf16[16,128,128]{2,1,0:T(8,128)(2,1)S(1)}, u32[]{:S(2)}, u32[]{:S(2)}) %collective-permute-start) | collective-permute-done | bytes 524320 | tf_op jit(solution)/shard_map/ppermute | solution.py:627
  19.6 14.2 %collective-permute-done.2.refs_5_ = bf16[16,128,128]{2,1,0:T(8,128)(2,1)S(1)} collective-permute-done((bf16[16,128,128]{2,1,0:T(8,128)(2,1)}, bf16[16,128,128]{2,1,0:T(8,128)(2,1)S(1)}, u32[]{:S(2)}, u32[]{:S(2)}) %collective-permute-start.2) | collective-permute-done | bytes 524320 | tf_op jit(solution)/shard_map/ppermute | solution.py:627
  33.8 21.4 %collective-permute-done.1.refs_4_ = bf16[16,128,128]{2,1,0:T(8,128)(2,1)S(1)} collective-permute-done((bf16[16,128,128]{2,1,0:T(8,128)(2,1)}, bf16[16,128,128]{2,1,0:T(8,128)(2,1)S(1)}, u32[]{:S(2)}, u32[]{:S(2)}) %collective-permute-start.1) | collective-permute-done | bytes 524320 | tf_op jit(solution)/shard_map/ppermute | solution.py:627
  55.1 0.6 collective-permute-start.3
  55.7 1.5 collective-permute-done.3
  57.2 0.7 maximum_select_fusion.refs_4_.table_ref
  57.9 11.9 %home_sweep.3.left_ref = f32[528,128]{1,0:T(8,128)} custom-call(f32[4]{0:T(128)} %temp_ref.5, bf16[2048,128]{1,0:T(8,128)(2,1)} %bitcast.29, bf16[2048,128]{1,0:T(8,128)(2,1)} %bitcast.20, bf16[2048,128]{1,0:T(8,128)(2,1)} %bitcast.26, bf16[2048,128]{1,0:T(8,128)(2,1)} %bitcast.23, f32[512,128]{1,0:T(8,128)} %maximum_select_fusion.refs_4_.table_ref), custom_call_target="tpu_custom_call" | custom-call | tf_op jit(solution)/shard_map/home_sweep/pallas_call | solution.py:544
  69.9 0.1 collective-permute-start.4
  70.0 3.6 %collective-permute-done.5.refs_0_.refs_1_ = s32[4,32]{1,0:T(4,128)S(1)} collective-permute-done((s32[4,32]{1,0:T(4,128)S(1)}, s32[4,32]{1,0:T(4,128)S(1)}, u32[]{:S(2)}, u32[]{:S(2)}) %collective-permute-start.5) | collective-permute-done | bytes 544 | tf_op jit(solution)/shard_map/ppermute | solution.py:627
  73.6 1.2 collective-permute-start.6
  74.8 5.8 %pack_values.1 = (bf16[4,6,128,128]{3,2,1,0:T(8,128)(2,1)}, bf16[4,6,128,128]{3,2,1,0:T(8,128)(2,1)}, bf16[4,6,128,128]{3,2,1,0:T(8,128)(2,1)}, bf16[4,48,128,128]{3,2,1,0:T(8,128)(2,1)}) custom-call(s32[4,32]{1,0:T(4,128)} %bitcast.35, bf16[4,32,128,128]{3,2,1,0:T(8,128)(2,1)} %bitcast.32), custom_call_target="tpu_custom_call" | custom-call | tf_op jit(solution)/shard_map/pack_values/pallas_call | solution.py:411
  80.6 2.1 collective-permute-start.25
  82.7 1.2 collective-permute-start.7
  83.9 6.1 %pack_keys.1 = (bf16[2,6,128,128]{3,2,1,0:T(8,128)(2,1)}, bf16[1,6,128,128]{3,2,1,0:T(8,128)(2,1)}, bf16[2,6,128,128]{3,2,1,0:T(8,128)(2,1)}, bf16[2,6,128,128]{3,2,1,0:T(8,128)(2,1)}, bf16[4,48,128,128]{3,2,1,0:T(8,128)(2,1)}) custom-call(s32[4,32]{1,0:T(4,128)} %bitcast.36, f32[4,32,128,128]{3,2,1,0:T(8,128)} %bitcast.19), custom_call_target="tpu_custom_call" | custom-call | tf_op jit(solution)/shard_map/pack_keys/pallas_call | solution.py:411
  89.9 2.0 home_renew.3.refs_4_.table_ref
  91.9 8.6 %collective-permute-done.7.refs_2_.refs_3_ = s32[4,32]{1,0:T(4,128)S(1)} collective-permute-done((s32[4,32]{1,0:T(4,128)S(1)}, s32[4,32]{1,0:T(4,128)S(1)}, u32[]{:S(2)}, u32[]{:S(2)}) %collective-permute-start.7) | collective-permute-done | bytes 544 | tf_op jit(solution)/shard_map/ppermute | solution.py:627
  100.5 0.6 copy-done.12
  101.0 0.2 copy-done.4
  101.3 3.8 %home_pages.1 = (bf16[4,48,128,128]{3,2,1,0:T(8,128)(2,1)}, bf16[12,128,128]{2,1,0:T(8,128)(2,1)}) custom-call(s32[4,32]{1,0:T(4,128)} %copy-done.10, s32[4,32]{1,0:T(4,128)} %copy-done.11, s32[4,32]{1,0:T(4,128)} %copy-done.12, bf16[16,128,128]{2,1,0:T(8,128)(2,1)} %copy-done.1, bf16[16,128,128]{2,1,0:T(8,128)(2,1)} %copy-done.3, ...), custom_call_target="tpu_custom_call", output_to_operand_aliasing={{0}: (9, {})} | custom-call | tf_op jit(solution)/shard_map/home_pages/pallas_call | solution.py:482
  105.0 12.0 %home_sweep.4.left_ref = f32[528,128]{1,0:T(8,128)} custom-call(f32[4]{0:T(128)} %temp_ref.5, bf16[2048,128]{1,0:T(8,128)(2,1)} %bitcast.30, bf16[2048,128]{1,0:T(8,128)(2,1)} %bitcast.21, bf16[2048,128]{1,0:T(8,128)(2,1)} %bitcast.27, bf16[2048,128]{1,0:T(8,128)(2,1)} %bitcast.24, f32[512,128]{1,0:T(8,128)} %home_renew.3.refs_4_.table_ref), custom_call_target="tpu_custom_call" | custom-call | tf_op jit(solution)/shard_map/home_sweep/pallas_call | solution.py:544
  117.0 2.7 %collective-permute-start.29 = (bf16[4,6,128,128]{3,2,1,0:T(8,128)(2,1)}, bf16[4,6,128,128]{3,2,1,0:T(8,128)(2,1)S(1)}, u32[]{:S(2)}, u32[]{:S(2)}) collective-permute-start(bf16[4,6,128,128]{3,2,1,0:T(8,128)(2,1)} %get-tuple-element.60), channel_id=1, source_target_pairs={{0,12},{4,8},{8,4},{12,0},{1,13},{5,9},{9,5},{13,1},{2,14},{6,10},... | collective-permute-start | bytes 2359304 | tf_op jit(solution)/shard_map/ppermute | solution.py:627
  119.7 0.8 collective-permute-start.15
  120.5 0.7 copy-done.7
  121.2 1.9 home_renew.4.refs_4_.table_ref
  123.2 12.1 %home_sweep.5.left_ref = f32[528,128]{1,0:T(8,128)} custom-call(f32[4]{0:T(128)} %temp_ref.5, bf16[2048,128]{1,0:T(8,128)(2,1)} %bitcast.31, bf16[2048,128]{1,0:T(8,128)(2,1)} %bitcast.22, bf16[2048,128]{1,0:T(8,128)(2,1)} %bitcast.28, bf16[2048,128]{1,0:T(8,128)(2,1)} %bitcast.25, f32[512,128]{1,0:T(8,128)} %home_renew.4.refs_4_.table_ref), custom_call_target="tpu_custom_call" | custom-call | tf_op jit(solution)/shard_map/home_sweep/pallas_call | solution.py:544
  135.3 5.2 %home_ids.1 = s32[4,48]{1,0:T(4,128)} custom-call(s32[4,32]{1,0:T(4,128)} %bitcast.37, s32[4,32]{1,0:T(4,128)} %copy-done.10, s32[4,32]{1,0:T(4,128)} %copy-done.11, s32[4,32]{1,0:T(4,128)} %copy-done.12), custom_call_target="tpu_custom_call" | custom-call | tf_op jit(solution)/shard_map/home_ids/pallas_call | solution.py:604
  140.5 1.2 collective-permute-start.19
  141.8 2.0 home_renew.5
  143.7 2.0 collective-permute-start.21
  145.8 0.9 constant_dynamic-update-slice_fusion.15
  146.7 13.9 %collective-permute-done.15 = bf16[2,6,128,128]{3,2,1,0:T(8,128)(2,1)S(1)} collective-permute-done((bf16[2,6,128,128]{3,2,1,0:T(8,128)(2,1)}, bf16[2,6,128,128]{3,2,1,0:T(8,128)(2,1)S(1)}, u32[]{:S(2)}, u32[]{:S(2)}) %collective-permute-start.15) | collective-permute-done | bytes 393248 | tf_op jit(solution)/shard_map/ppermute | solution.py:627
  160.6 3.6 %collective-permute-start.13 = (f32[256,128]{1,0:T(8,128)S(1)}, f32[256,128]{1,0:T(8,128)S(1)}, u32[]{:S(2)}, u32[]{:S(2)}) collective-permute-start(f32[256,128]{1,0:T(8,128)S(1)} %get-tuple-element.63), channel_id=1, source_target_pairs={{0,8},{4,12},{8,0},{12,4},{1,9},{5,13},{9,1},{13,5},{2,10},{6,14},... | collective-permute-start | bytes 393224 | tf_op jit(solution)/shard_map/ppermute | solution.py:627
  164.2 1.0 constant_dynamic-update-slice_fusion.5
  165.2 45.9 %collective-permute-done.13 = f32[256,128]{1,0:T(8,128)S(1)} collective-permute-done((f32[256,128]{1,0:T(8,128)S(1)}, f32[256,128]{1,0:T(8,128)S(1)}, u32[]{:S(2)}, u32[]{:S(2)}) %collective-permute-start.13) | collective-permute-done | bytes 131104 | tf_op jit(solution)/shard_map/ppermute | solution.py:627
  211.2 2.1 collective-permute-start.14
  213.3 0.8 constant_dynamic-update-slice_fusion.13
  214.1 5.0 %collective-permute-done.17 = bf16[1,6,128,128]{3,2,1,0:T(8,128)(2,1)S(1)} collective-permute-done((bf16[1,6,128,128]{3,2,1,0:T(8,128)(2,1)}, bf16[1,6,128,128]{3,2,1,0:T(8,128)(2,1)S(1)}, u32[]{:S(2)}, u32[]{:S(2)}) %collective-permute-start.17) | collective-permute-done | bytes 196640 | tf_op jit(solution)/shard_map/ppermute | solution.py:627
  219.1 0.5 collective-permute-start.28
  219.6 0.1 collective-permute-start.18
  219.7 4.1 %collective-permute-done.14 = f32[2,256,128]{2,1,0:T(8,128)S(1)} collective-permute-done((f32[2,256,128]{2,1,0:T(8,128)S(1)}, f32[2,256,128]{2,1,0:T(8,128)S(1)}, u32[]{:S(2)}, u32[]{:S(2)}) %collective-permute-start.14) | collective-permute-done | bytes 262176 | tf_op jit(solution)/shard_map/ppermute | solution.py:627
  223.9 1.3 collective-permute-start.23
  225.2 0.8 constant_dynamic-update-slice_fusion.12
  226.0 0.7 constant_dynamic-update-slice_fusion.11
  226.7 0.2 collective-permute-start.22
  226.9 0.7 constant_dynamic-update-slice_fusion.10
  227.6 1.8 constant_dynamic-update-slice_fusion.9
  229.4 8.2 %collective-permute-done.23 = bf16[2,6,128,128]{3,2,1,0:T(8,128)(2,1)S(1)} collective-permute-done((bf16[2,6,128,128]{3,2,1,0:T(8,128)(2,1)}, bf16[2,6,128,128]{3,2,1,0:T(8,128)(2,1)S(1)}, u32[]{:S(2)}, u32[]{:S(2)}) %collective-permute-start.23) | collective-permute-done | bytes 393248 | tf_op jit(solution)/shard_map/ppermute | solution.py:627
  237.6 0.5 collective-permute-start.24
  238.1 0.8 constant_dynamic-update-slice_fusion.8
  238.9 0.8 bitcast_dynamic-update-slice_fusion.1
  239.7 0.8 bitcast_dynamic-update-slice_fusion
  240.4 0.8 constant_dynamic-update-slice_fusion.7
  241.2 1.1 constant_dynamic-update-slice_fusion.4
  242.3 1.0 constant_dynamic-update-slice_fusion.3
  243.3 1.1 constant_dynamic-update-slice_fusion.2
  244.4 1.0 constant_dynamic-update-slice_fusion.1
  245.4 1.1 constant_dynamic-update-slice_fusion
  246.5 0.8 constant_dynamic-update-slice_fusion.6
  (59 shorter events, 0.2 us)
Async XLA Ops:
  0.6 54.5 %copy-start = (f32[4,256,128]{2,1,0:T(8,128)S(1)}, f32[4,256,128]{2,1,0:T(8,128)}, u32[]{:S(2)}) copy-start(f32[4,256,128]{2,1,0:T(8,128)} %param.7) | copy-start | bytes 1572868
  0.6 69.4 %copy-start.8 = (s32[4,32,1]{1,2,0:T(1,128)S(1)}, s32[4,32,1]{1,2,0:T(1,128)}, u32[]{:S(2)}) copy-start(s32[4,32,1]{1,2,0:T(1,128)} %param.9) | copy-start | bytes 1540
  0.7 82.0 %copy-start.9 = (s32[4,32,1]{1,2,0:T(1,128)S(1)}, s32[4,32,1]{1,2,0:T(1,128)}, u32[]{:S(2)}) copy-start(s32[4,32,1]{1,2,0:T(1,128)} %param.9) | copy-start | bytes 1540
  3.8 15.7 %collective-permute-start = (bf16[16,128,128]{2,1,0:T(8,128)(2,1)}, bf16[16,128,128]{2,1,0:T(8,128)(2,1)S(1)}, u32[]{:S(2)}, u32[]{:S(2)}) collective-permute-start(bf16[16,128,128]{2,1,0:T(8,128)(2,1)} %get-tuple-element.34), channel_id=1, source_target_pairs={{0,4},{4,0},{8,12},{12,8},{1,5},{5,1},{9,13},{13,9},{2,6},{6,2},{1... | collective-permute-start | bytes 1572872 | tf_op jit(solution)/shard_map/ppermute | solution.py:627
  7.0 26.8 %collective-permute-start.2 = (bf16[16,128,128]{2,1,0:T(8,128)(2,1)}, bf16[16,128,128]{2,1,0:T(8,128)(2,1)S(1)}, u32[]{:S(2)}, u32[]{:S(2)}) collective-permute-start(bf16[16,128,128]{2,1,0:T(8,128)(2,1)} %get-tuple-element.36), channel_id=1, source_target_pairs={{0,12},{4,8},{8,4},{12,0},{1,13},{5,9},{9,5},{13,1},{2,14},{6,10},... | collective-permute-start | bytes 1572872 | tf_op jit(solution)/shard_map/ppermute | solution.py:627
  9.4 45.7 %collective-permute-start.1 = (bf16[16,128,128]{2,1,0:T(8,128)(2,1)}, bf16[16,128,128]{2,1,0:T(8,128)(2,1)S(1)}, u32[]{:S(2)}, u32[]{:S(2)}) collective-permute-start(bf16[16,128,128]{2,1,0:T(8,128)(2,1)} %get-tuple-element.35), channel_id=1, source_target_pairs={{0,8},{4,12},{8,0},{12,4},{1,9},{5,13},{9,1},{13,5},{2,10},{6,14},... | collective-permute-start | bytes 1572872 | tf_op jit(solution)/shard_map/ppermute | solution.py:627
  19.6 38.3 %copy-start.1 = (bf16[16,128,128]{2,1,0:T(8,128)(2,1)}, bf16[16,128,128]{2,1,0:T(8,128)(2,1)S(1)}, u32[]{:S(2)}) copy-start(bf16[16,128,128]{2,1,0:T(8,128)(2,1)S(1)} %collective-permute-done.refs_3_) | copy-start | bytes 1572868
  19.6 80.9 %collective-permute-start.8 = (bf16[16,128,128]{2,1,0:T(8,128)(2,1)S(1)}, bf16[16,128,128]{2,1,0:T(8,128)(2,1)S(1)}, u32[]{:S(2)}, u32[]{:S(2)}) collective-permute-start(bf16[16,128,128]{2,1,0:T(8,128)(2,1)S(1)} %collective-permute-done.refs_3_), channel_id=1, source_target_pairs={{0,1},{1,0},{2,3},{3,2},{4,5},{5,4},{6,7},{7,6},{8,9},{9,8},{10,11... | collective-permute-start | bytes 1572872 | tf_op jit(solution)/shard_map/ppermute | solution.py:624
  33.7 24.2 %copy-start.2 = (bf16[16,128,128]{2,1,0:T(8,128)(2,1)}, bf16[16,128,128]{2,1,0:T(8,128)(2,1)S(1)}, u32[]{:S(2)}) copy-start(bf16[16,128,128]{2,1,0:T(8,128)(2,1)S(1)} %collective-permute-done.2.refs_5_) | copy-start | bytes 1572868
  33.7 66.7 %collective-permute-start.10 = (bf16[16,128,128]{2,1,0:T(8,128)(2,1)S(1)}, bf16[16,128,128]{2,1,0:T(8,128)(2,1)}, u32[]{:S(2)}, u32[]{:S(2)}) collective-permute-start(bf16[16,128,128]{2,1,0:T(8,128)(2,1)S(1)} %collective-permute-done.2.refs_5_), channel_id=1, source_target_pairs={{0,1},{1,0},{2,3},{3,2},{4,5},{5,4},{6,7},{7,6},{8,9},{9,8},{10,11... | collective-permute-start | bytes 1572872 | tf_op jit(solution)/shard_map/ppermute | solution.py:624
  55.1 2.8 %copy-start.3 = (bf16[16,128,128]{2,1,0:T(8,128)(2,1)}, bf16[16,128,128]{2,1,0:T(8,128)(2,1)S(1)}, u32[]{:S(2)}) copy-start(bf16[16,128,128]{2,1,0:T(8,128)(2,1)S(1)} %collective-permute-done.1.refs_4_) | copy-start | bytes 1572868
  55.1 45.4 %collective-permute-start.9 = (bf16[16,128,128]{2,1,0:T(8,128)(2,1)S(1)}, bf16[16,128,128]{2,1,0:T(8,128)(2,1)}, u32[]{:S(2)}, u32[]{:S(2)}) collective-permute-start(bf16[16,128,128]{2,1,0:T(8,128)(2,1)S(1)} %collective-permute-done.1.refs_4_), channel_id=1, source_target_pairs={{0,1},{1,0},{2,3},{3,2},{4,5},{5,4},{6,7},{7,6},{8,9},{9,8},{10,11... | collective-permute-start | bytes 1572872 | tf_op jit(solution)/shard_map/ppermute | solution.py:624
  55.1 2.1 collective-permute-start.3
  69.9 12.8 %collective-permute-start.4 = (f32[528,128]{1,0:T(8,128)}, f32[528,128]{1,0:T(8,128)}, u32[]{:S(2)}, u32[]{:S(2)}) collective-permute-start(f32[528,128]{1,0:T(8,128)} %home_sweep.3.left_ref), channel_id=1, source_target_pairs={{0,1},{1,0},{2,3},{3,2},{4,5},{5,4},{6,7},{7,6},{8,9},{9,8},{10,11... | collective-permute-start | bytes 811016 | tf_op jit(solution)/shard_map/ppermute | solution.py:624
  70.0 3.6 %collective-permute-start.5 = (s32[4,32]{1,0:T(4,128)S(1)}, s32[4,32]{1,0:T(4,128)S(1)}, u32[]{:S(2)}, u32[]{:S(2)}) collective-permute-start(s32[4,32]{1,0:T(4,128)S(1)} %bitcast.38), channel_id=1, source_target_pairs={{0,4},{4,0},{8,12},{12,8},{1,5},{5,1},{9,13},{13,9},{2,6},{6,2},{1... | collective-permute-start | bytes 1544 | tf_op jit(solution)/shard_map/ppermute | solution.py:627
  73.6 16.3 %copy-start.10 = (s32[4,32]{1,0:T(4,128)}, s32[4,32]{1,0:T(4,128)S(1)}, u32[]{:S(2)}) copy-start(s32[4,32]{1,0:T(4,128)S(1)} %collective-permute-done.5.refs_0_.refs_1_) | copy-start | bytes 1540
  73.6 7.0 %collective-permute-start.6 = (s32[4,32]{1,0:T(4,128)S(1)}, s32[4,32]{1,0:T(4,128)S(1)}, u32[]{:S(2)}, u32[]{:S(2)}) collective-permute-start(s32[4,32]{1,0:T(4,128)S(1)} %bitcast.39), channel_id=1, source_target_pairs={{0,8},{4,12},{8,0},{12,4},{1,9},{5,13},{9,1},{13,5},{2,10},{6,14},... | collective-permute-start | bytes 1544 | tf_op jit(solution)/shard_map/ppermute | solution.py:627
  80.6 19.9 %copy-start.11 = (s32[4,32]{1,0:T(4,128)}, s32[4,32]{1,0:T(4,128)S(1)}, u32[]{:S(2)}) copy-start(s32[4,32]{1,0:T(4,128)S(1)} %collective-permute-done.6.refs_1_.refs_2_) | copy-start | bytes 1540
  80.6 63.2 %collective-permute-start.25 = (bf16[4,6,128,128]{3,2,1,0:T(8,128)(2,1)}, bf16[4,6,128,128]{3,2,1,0:T(8,128)(2,1)S(1)}, u32[]{:S(2)}, u32[]{:S(2)}) collective-permute-start(bf16[4,6,128,128]{3,2,1,0:T(8,128)(2,1)} %get-tuple-element.39), channel_id=1, source_target_pairs={{0,4},{4,0},{8,12},{12,8},{1,5},{5,1},{9,13},{13,9},{2,6},{6,2},{1... | collective-permute-start | bytes 2359304 | tf_op jit(solution)/shard_map/ppermute | solution.py:627
  82.7 17.8 %collective-permute-start.7 = (s32[4,32]{1,0:T(4,128)S(1)}, s32[4,32]{1,0:T(4,128)S(1)}, u32[]{:S(2)}, u32[]{:S(2)}) collective-permute-start(s32[4,32]{1,0:T(4,128)S(1)} %bitcast.40), channel_id=1, source_target_pairs={{0,12},{4,8},{8,4},{12,0},{1,13},{5,9},{9,5},{13,1},{2,14},{6,10},... | collective-permute-start | bytes 1544 | tf_op jit(solution)/shard_map/ppermute | solution.py:627
  100.5 0.6 copy-start.12
  100.5 0.8 copy-start.4
  117.0 3.5 %collective-permute-start.11 = (f32[528,128]{1,0:T(8,128)}, f32[528,128]{1,0:T(8,128)S(1)}, u32[]{:S(2)}, u32[]{:S(2)}) collective-permute-start(f32[528,128]{1,0:T(8,128)} %home_sweep.4.left_ref), channel_id=1, source_target_pairs={{0,1},{1,0},{2,3},{3,2},{4,5},{5,4},{6,7},{7,6},{8,9},{9,8},{10,11... | collective-permute-start | bytes 811016 | tf_op jit(solution)/shard_map/ppermute | solution.py:624
  117.0 94.2 %collective-permute-start.27 = (bf16[4,6,128,128]{3,2,1,0:T(8,128)(2,1)}, bf16[4,6,128,128]{3,2,1,0:T(8,128)(2,1)S(1)}, u32[]{:S(2)}, u32[]{:S(2)}) collective-permute-start(bf16[4,6,128,128]{3,2,1,0:T(8,128)(2,1)} %get-tuple-element.58), channel_id=1, source_target_pairs={{0,8},{4,12},{8,0},{12,4},{1,9},{5,13},{9,1},{13,5},{2,10},{6,14},... | collective-permute-start | bytes 2359304 | tf_op jit(solution)/shard_map/ppermute | solution.py:627
  117.0 97.1 %collective-permute-start.29 = (bf16[4,6,128,128]{3,2,1,0:T(8,128)(2,1)}, bf16[4,6,128,128]{3,2,1,0:T(8,128)(2,1)S(1)}, u32[]{:S(2)}, u32[]{:S(2)}) collective-permute-start(bf16[4,6,128,128]{3,2,1,0:T(8,128)(2,1)} %get-tuple-element.60), channel_id=1, source_target_pairs={{0,12},{4,8},{8,4},{12,0},{1,13},{5,9},{9,5},{13,1},{2,14},{6,10},... | collective-permute-start | bytes 2359304 | tf_op jit(solution)/shard_map/ppermute | solution.py:627
  119.7 40.9 %collective-permute-start.15 = (bf16[2,6,128,128]{3,2,1,0:T(8,128)(2,1)}, bf16[2,6,128,128]{3,2,1,0:T(8,128)(2,1)S(1)}, u32[]{:S(2)}, u32[]{:S(2)}) collective-permute-start(bf16[2,6,128,128]{3,2,1,0:T(8,128)(2,1)} %get-tuple-element.46), channel_id=1, source_target_pairs={{0,4},{4,0},{8,12},{12,8},{1,5},{5,1},{9,13},{13,9},{2,6},{6,2},{1... | collective-permute-start | bytes 1179656 | tf_op jit(solution)/shard_map/ppermute | solution.py:627
  120.5 0.7 copy-start.7
  135.3 5.2 %collective-permute-start.12 = (f32[528,128]{1,0:T(8,128)}, f32[528,128]{1,0:T(8,128)S(1)}, u32[]{:S(2)}, u32[]{:S(2)}) collective-permute-start(f32[528,128]{1,0:T(8,128)} %home_sweep.5.left_ref), channel_id=1, source_target_pairs={{0,1},{1,0},{2,3},{3,2},{4,5},{5,4},{6,7},{7,6},{8,9},{9,8},{10,11... | collective-permute-start | bytes 811016 | tf_op jit(solution)/shard_map/ppermute | solution.py:624
  140.5 1.3 copy-start.6
  140.5 78.6 %collective-permute-start.19 = (bf16[2,6,128,128]{3,2,1,0:T(8,128)(2,1)}, bf16[2,6,128,128]{3,2,1,0:T(8,128)(2,1)}, u32[]{:S(2)}, u32[]{:S(2)}) collective-permute-start(bf16[2,6,128,128]{3,2,1,0:T(8,128)(2,1)} %get-tuple-element.50), channel_id=1, source_target_pairs={{0,8},{4,12},{8,0},{12,4},{1,9},{5,13},{9,1},{13,5},{2,10},{6,14},... | collective-permute-start | bytes 1179656 | tf_op jit(solution)/shard_map/ppermute | solution.py:627
  143.7 75.9 %collective-permute-start.21 = (bf16[12,128,128]{2,1,0:T(8,128)(2,1)}, bf16[12,128,128]{2,1,0:T(8,128)(2,1)S(1)}, u32[]{:S(2)}, u32[]{:S(2)}) collective-permute-start(bf16[12,128,128]{2,1,0:T(8,128)(2,1)} %get-tuple-element.43), channel_id=1, source_target_pairs={{0,4},{4,0},{8,12},{12,8},{1,5},{5,1},{9,13},{13,9},{2,6},{6,2},{1... | collective-permute-start | bytes 1179656 | tf_op jit(solution)/shard_map/ppermute | solution.py:627
  160.6 50.5 %collective-permute-start.13 = (f32[256,128]{1,0:T(8,128)S(1)}, f32[256,128]{1,0:T(8,128)S(1)}, u32[]{:S(2)}, u32[]{:S(2)}) collective-permute-start(f32[256,128]{1,0:T(8,128)S(1)} %get-tuple-element.63), channel_id=1, source_target_pairs={{0,8},{4,12},{8,0},{12,4},{1,9},{5,13},{9,1},{13,5},{2,10},{6,14},... | collective-permute-start | bytes 393224 | tf_op jit(solution)/shard_map/ppermute | solution.py:627
  211.1 8.0 %collective-permute-start.17 = (bf16[1,6,128,128]{3,2,1,0:T(8,128)(2,1)}, bf16[1,6,128,128]{3,2,1,0:T(8,128)(2,1)S(1)}, u32[]{:S(2)}, u32[]{:S(2)}) collective-permute-start(bf16[1,6,128,128]{3,2,1,0:T(8,128)(2,1)} %get-tuple-element.48), channel_id=1, source_target_pairs={{0,4},{4,0},{8,12},{12,8},{1,5},{5,1},{9,13},{13,9},{2,6},{6,2},{1... | collective-permute-start | bytes 589832 | tf_op jit(solution)/shard_map/ppermute | solution.py:627
  211.2 12.6 %collective-permute-start.14 = (f32[2,256,128]{2,1,0:T(8,128)S(1)}, f32[2,256,128]{2,1,0:T(8,128)S(1)}, u32[]{:S(2)}, u32[]{:S(2)}) collective-permute-start(f32[2,256,128]{2,1,0:T(8,128)S(1)} %pad_maximum_fusion), channel_id=1, source_target_pairs={{0,4},{4,0},{8,12},{12,8},{1,5},{5,1},{9,13},{13,9},{2,6},{6,2},{1... | collective-permute-start | bytes 786440 | tf_op jit(solution)/shard_map/ppermute | solution.py:627
  214.1 27.2 %collective-permute-start.26 = (bf16[4,6,128,128]{3,2,1,0:T(8,128)(2,1)S(1)}, bf16[4,6,128,128]{3,2,1,0:T(8,128)(2,1)S(1)}, u32[]{:S(2)}, u32[]{:S(2)}) collective-permute-start(bf16[4,6,128,128]{3,2,1,0:T(8,128)(2,1)S(1)} %collective-permute-done.25), channel_id=1, source_target_pairs={{0,1},{1,0},{2,3},{3,2},{4,5},{5,4},{6,7},{7,6},{8,9},{9,8},{10,11... | collective-permute-start | bytes 2359304 | tf_op jit(solution)/shard_map/ppermute | solution.py:624
  219.1 4.7 %collective-permute-start.16 = (bf16[2,6,128,128]{3,2,1,0:T(8,128)(2,1)S(1)}, bf16[2,6,128,128]{3,2,1,0:T(8,128)(2,1)S(1)}, u32[]{:S(2)}, u32[]{:S(2)}) collective-permute-start(bf16[2,6,128,128]{3,2,1,0:T(8,128)(2,1)S(1)} %collective-permute-done.15), channel_id=1, source_target_pairs={{0,1},{1,0},{2,3},{3,2},{4,5},{5,4},{6,7},{7,6},{8,9},{9,8},{10,11... | collective-permute-start | bytes 1179656 | tf_op jit(solution)/shard_map/ppermute | solution.py:624
  219.1 24.2 %collective-permute-start.28 = (bf16[4,6,128,128]{3,2,1,0:T(8,128)(2,1)S(1)}, bf16[4,6,128,128]{3,2,1,0:T(8,128)(2,1)S(1)}, u32[]{:S(2)}, u32[]{:S(2)}) collective-permute-start(bf16[4,6,128,128]{3,2,1,0:T(8,128)(2,1)S(1)} %collective-permute-done.27), channel_id=1, source_target_pairs={{0,1},{1,0},{2,3},{3,2},{4,5},{5,4},{6,7},{7,6},{8,9},{9,8},{10,11... | collective-permute-start | bytes 2359304 | tf_op jit(solution)/shard_map/ppermute | solution.py:624
  219.6 7.0 %collective-permute-start.18 = (bf16[1,6,128,128]{3,2,1,0:T(8,128)(2,1)S(1)}, bf16[1,6,128,128]{3,2,1,0:T(8,128)(2,1)S(1)}, u32[]{:S(2)}, u32[]{:S(2)}) collective-permute-start(bf16[1,6,128,128]{3,2,1,0:T(8,128)(2,1)S(1)} %collective-permute-done.17), channel_id=1, source_target_pairs={{0,1},{1,0},{2,3},{3,2},{4,5},{5,4},{6,7},{7,6},{8,9},{9,8},{10,11... | collective-permute-start | bytes 589832 | tf_op jit(solution)/shard_map/ppermute | solution.py:624
  223.8 13.8 %collective-permute-start.20 = (bf16[2,6,128,128]{3,2,1,0:T(8,128)(2,1)}, bf16[2,6,128,128]{3,2,1,0:T(8,128)(2,1)S(1)}, u32[]{:S(2)}, u32[]{:S(2)}) collective-permute-start(bf16[2,6,128,128]{3,2,1,0:T(8,128)(2,1)} %collective-permute-done.19), channel_id=1, source_target_pairs={{0,1},{1,0},{2,3},{3,2},{4,5},{5,4},{6,7},{7,6},{8,9},{9,8},{10,11... | collective-permute-start | bytes 1179656 | tf_op jit(solution)/shard_map/ppermute | solution.py:624
  223.8 22.7 %copy-start.5 = (f32[4,256,128]{2,1,0:T(8,128)}, f32[4,256,128]{2,1,0:T(8,128)S(1)}, u32[]{:S(2)}) copy-start(f32[4,256,128]{2,1,0:T(8,128)S(1)} %slice_dynamic-update-slice_fusion) | copy-start | bytes 1572868
  223.9 13.7 %collective-permute-start.23 = (bf16[2,6,128,128]{3,2,1,0:T(8,128)(2,1)}, bf16[2,6,128,128]{3,2,1,0:T(8,128)(2,1)S(1)}, u32[]{:S(2)}, u32[]{:S(2)}) collective-permute-start(bf16[2,6,128,128]{3,2,1,0:T(8,128)(2,1)} %get-tuple-element.54), channel_id=1, source_target_pairs={{0,12},{4,8},{8,4},{12,0},{1,13},{5,9},{9,5},{13,1},{2,14},{6,10},... | collective-permute-start | bytes 1179656 | tf_op jit(solution)/shard_map/ppermute | solution.py:627
  226.7 13.0 %collective-permute-start.22 = (bf16[12,128,128]{2,1,0:T(8,128)(2,1)S(1)}, bf16[12,128,128]{2,1,0:T(8,128)(2,1)S(1)}, u32[]{:S(2)}, u32[]{:S(2)}) collective-permute-start(bf16[12,128,128]{2,1,0:T(8,128)(2,1)S(1)} %collective-permute-done.21), channel_id=1, source_target_pairs={{0,1},{1,0},{2,3},{3,2},{4,5},{5,4},{6,7},{7,6},{8,9},{9,8},{10,11... | collective-permute-start | bytes 1179656 | tf_op jit(solution)/shard_map/ppermute | solution.py:624
  237.6 7.9 %collective-permute-start.30 = (bf16[4,6,128,128]{3,2,1,0:T(8,128)(2,1)S(1)}, bf16[4,6,128,128]{3,2,1,0:T(8,128)(2,1)S(1)}, u32[]{:S(2)}, u32[]{:S(2)}) collective-permute-start(bf16[4,6,128,128]{3,2,1,0:T(8,128)(2,1)S(1)} %collective-permute-done.29), channel_id=1, source_target_pairs={{0,1},{1,0},{2,3},{3,2},{4,5},{5,4},{6,7},{7,6},{8,9},{9,8},{10,11... | collective-permute-start | bytes 2359304 | tf_op jit(solution)/shard_map/ppermute | solution.py:624
  237.6 9.0 %collective-permute-start.24 = (bf16[2,6,128,128]{3,2,1,0:T(8,128)(2,1)S(1)}, bf16[2,6,128,128]{3,2,1,0:T(8,128)(2,1)S(1)}, u32[]{:S(2)}, u32[]{:S(2)}) collective-permute-start(bf16[2,6,128,128]{3,2,1,0:T(8,128)(2,1)S(1)} %collective-permute-done.23), channel_id=1, source_target_pairs={{0,1},{1,0},{2,3},{3,2},{4,5},{5,4},{6,7},{7,6},{8,9},{9,8},{10,11... | collective-permute-start | bytes 1179656 | tf_op jit(solution)/shard_map/ppermute | solution.py:624
